TPU v7x, 128 devices: a whole 4x4x4 slice. The times are simulated.
128 devices in a mesh: section: 8 (over z, x_lo), dp: 16 (over y, x_hi, core).
Axes of the slice: x: 4 (x_hi: 2, x_lo: 2; x = x_hi * 2 + x_lo), y: 4, z: 4, core: 2. Of those that a mesh axis runs over, the one named last changes fastest.
Arguments:
- master: float32 [8, 2560, 2560], P('section', 'dp'), may hold values from -0.125 to 0.125
- first_moment: float32 [8, 2560, 2560], P('section', 'dp'), may hold values from -3 to 3
- second_moment: float32 [8, 2560, 2560], P('section', 'dp'), may hold values from 0.1 to 4
- inputs_own: bfloat16 [8, 4, 2048, 2560], P('section', None, 'dp'), may hold values from -6 to 6
- inputs_arriving: bfloat16 [8, 4, 2048, 2560], P('section', None, 'dp'), may hold values from -6 to 6
- grads_own: bfloat16 [8, 4, 2048, 2560], P('section', None, 'dp'), may hold values from -0.13183594 to 0.13183594
- windows_own: int32 [8, 2048, 2560], P('section', 'dp'), may hold values from 0 to 15
- windows_arriving: int32 [8, 2048, 2560], P('section', 'dp'), may hold values from 0 to 15
- next_inputs: bfloat16 [8, 512, 2560], P('section', 'dp'), may hold values from -6 to 6
Outputs:
- fresh_params: float32 [8, 2560, 2560], P('section', 'dp')
- fresh_first: float32 [8, 2560, 2560], P('section', 'dp')
- fresh_second: float32 [8, 2560, 2560], P('section', 'dp')
- next_currents: bfloat16 [8, 512, 2560], P('section', 'dp')
Inputs may be any that keep to these rules, and one draw needn't show every extreme that they name: `windows_own`: bit t of an entry is the surrogate derivative of spikes_t by v_t for timestep t. `windows_arriving`: bit t of an entry is the surrogate derivative of spikes_t by v_t for timestep t.
All inputs are finite; a program needn't handle non-finite values.
Results may differ from a plain program's by a relative error of at most 0.008.
Values may be sent and summed in bfloat16 or wider, within the bound.
A program may use at most 128 MiB of HBM per device.

v0:
```python
import jax
import jax.numpy as jnp
from jax import lax
from jax.sharding import PartitionSpec as P

LEAK_RATE = 0.5
LEARN_RATE = 0.002
FIRST_DECAY = 0.9
SECOND_DECAY = 0.95
EPSILON = 1e-08
WEIGHT_DECAY = 0.1
FIRST_CORRECTION = 1.0 - 0.9**10
SECOND_CORRECTION = 1.0 - 0.95**10


def passed_along(shard, axis, by):
    count = lax.axis_size(axis)
    pairs = [(i, i + by) for i in range(count) if 0 <= i + by < count]
    return lax.ppermute(shard, axis, pairs)


def membrane_grads(gradients, windows):
    carried = jnp.zeros(gradients.shape[1:], jnp.float32)
    results = []
    for moment in reversed(range(gradients.shape[0])):
        window = jnp.bitwise_and(jnp.right_shift(windows, moment), 1).astype(jnp.float32)
        carried = window * gradients[moment].astype(jnp.float32) + LEAK_RATE * carried
        results = [carried] + results
    return jnp.stack(results).astype(jnp.bfloat16)


def shards(
    master,
    first_moment,
    second_moment,
    inputs_own,
    inputs_arriving,
    grads_own,
    windows_own,
    windows_arriving,
    next_inputs,
):
    params = master[0]
    timesteps, tok_rows, features = (grads_own.shape[1], grads_own.shape[2], grads_own.shape[3])
    flat_rows = timesteps * tok_rows
    membrane_own = membrane_grads(grads_own[0], windows_own[0]).reshape(flat_rows, features)
    through = lax.dot_general(
        membrane_own,
        lax.all_gather(params.astype(jnp.bfloat16), "dp", axis=0, tiled=True),
        (((1,), (1,)), ((), ())),
        preferred_element_type=jnp.float32,
    )
    outgoing = (grads_own[0].reshape(flat_rows, features).astype(jnp.float32) + through).astype(
        jnp.bfloat16
    )
    received = passed_along(outgoing.reshape(timesteps, tok_rows, features), "section", -1)
    membrane_arriving = membrane_grads(received, windows_arriving[0]).reshape(flat_rows, features)
    acts_own = inputs_own[0].reshape(flat_rows, features)
    acts_arriving = inputs_arriving[0].reshape(flat_rows, features)
    contract = (((0,), (0,)), ((), ()))
    partial_value = lax.dot_general(
        acts_own, membrane_own, contract, preferred_element_type=jnp.float32
    )
    gradient = lax.psum_scatter(
        (
            partial_value
            + lax.dot_general(
                acts_arriving, membrane_arriving, contract, preferred_element_type=jnp.float32
            )
        ).astype(jnp.bfloat16),
        "dp",
        scatter_dimension=0,
        tiled=True,
    ).astype(jnp.float32)
    fresh_first = FIRST_DECAY * first_moment[0] + (1.0 - FIRST_DECAY) * gradient
    fresh_second = SECOND_DECAY * second_moment[0] + (1.0 - SECOND_DECAY) * gradient * gradient
    direction = (
        fresh_first / FIRST_CORRECTION / (jnp.sqrt(fresh_second / SECOND_CORRECTION) + EPSILON)
    )
    fresh_params = params - LEARN_RATE * (direction + WEIGHT_DECAY * params)
    fresh_weights = fresh_params.astype(jnp.bfloat16)
    upcoming = next_inputs[0]
    currents = jnp.dot(
        upcoming,
        lax.all_gather(fresh_weights, "dp", axis=0, tiled=True),
        preferred_element_type=jnp.float32,
    )
    next_currents = currents.astype(jnp.bfloat16)
    return (fresh_params[None], fresh_first[None], fresh_second[None], next_currents[None])


def solution(mesh):
    return jax.shard_map(
        shards,
        mesh=mesh,
        in_specs=(
            P("section", "dp", None),
            P("section", "dp", None),
            P("section", "dp", None),
            P("section", None, "dp", None),
            P("section", None, "dp", None),
            P("section", None, "dp", None),
            P("section", "dp", None),
            P("section", "dp", None),
            P("section", "dp", None),
        ),
        out_specs=(
            P("section", "dp", None),
            P("section", "dp", None),
            P("section", "dp", None),
            P("section", "dp", None),
        ),
        check_vma=False,
    )
```

profile of v0, /device:TPU:1, one launch (start us, length us, event | category | flops | bytes accessed | tf_op | source)
XLA Modules:
  0.0 454.4 jit_solution(939705589628608496)
XLA Ops:
  7.2 0.0 copy-start
  7.2 0.0 all-gather.3.cloned.1.call-start
  7.2 2.6 bitcast_convert_fusion
  9.8 0.0 all-gather.3.cloned.1.call-update
  9.8 0.0 reduce-scatter.4.cloned.1.call-start
  9.9 3.2 fusion.9
  13.1 1.8 maximum_convert_fusion
  14.9 92.3 %all-gather.3.cloned.1.call-done = bf16[2560,2560]{1,0:T(8,128)(2,1)} async-done(((bf16[160,2560]{1,0:T(8,128)(2,1)}), bf16[2560,2560]{1,0:T(8,128)(2,1)}) %all-gather.3.cloned.1.call-update) | async-done | bytes 13107216 | tf_op jit(solution)/shard_map/all_gather | solution.py:49
  107.2 13.9 %fusion.1 = bf16[512,2560]{1,0:T(8,128)(2,1)} fusion(bf16[512,2560]{1,0:T(8,128)(2,1)} %bitcast.79, bf16[512,2560]{1,0:T(8,128)(2,1)} %bitcast.80, bf16[2560,2560]{1,0:T(8,128)(2,1)} %all-gather.3.cloned.1.call-done), kind=kOutput, calls=%fused_computation.4 | convolution fusion | flops 6714818560 | bytes 20971520 | tf_op jit(solution)/shard_map/dot_general | solution.py:47
  121.1 1.5 collective-permute-start
  122.6 12.3 %fusion.17 = f32[2560,2560]{1,0:T(8,128)} fusion(bf16[512,2560]{1,0:T(8,128)(2,1)S(1)} %bitcast.81, bf16[512,2560]{1,0:T(8,128)(2,1)S(1)} %bitcast.78), kind=kOutput, calls=%fused_computation.35 | convolution fusion | flops 6710886400 | bytes 31457280 | tf_op jit(solution)/shard_map/dot_general | solution.py:61
  134.9 46.4 %collective-permute-done = bf16[4,128,2560]{2,1,0:T(8,128)(2,1)S(1)} collective-permute-done((bf16[4,128,2560]{2,1,0:T(8,128)(2,1)}, bf16[4,128,2560]{2,1,0:T(8,128)(2,1)S(1)}, u32[]{:S(2)}, u32[]{:S(2)}) %collective-permute-start) | collective-permute-done | bytes 2621472 | tf_op jit(solution)/shard_map/ppermute | solution.py:19
  181.4 1.2 add_convert_fusion.1
  182.5 1.8 pad_maximum_fusion
  184.4 16.4 %fusion = bf16[2560,2560]{0,1:T(8,128)(2,1)} fusion(f32[2560,2560]{1,0:T(8,128)} %fusion.17, bf16[512,2560]{1,0:T(8,128)(2,1)} %bitcast.82, bf16[512,2560]{1,0:T(8,128)(2,1)} %bitcast.84), kind=kOutput, calls=%fused_computation.1 | convolution fusion | flops 6723993600 | bytes 44564480 | tf_op jit(solution)/shard_map/dot_general | solution.py:67
  200.8 17.7 %copy.20 = bf16[2560,2560]{1,0:T(8,128)(2,1)} copy(bf16[2560,2560]{0,1:T(8,128)(2,1)} %fusion) | data formatting | bytes 26214400
  218.4 0.0 reduce-scatter.4.cloned.1.call-update
  218.5 0.0 copy-start.5
  218.5 0.0 all-gather.5.cloned.1.call-start
  218.5 123.0 %reduce-scatter.4.cloned.1.call-done = bf16[160,2560]{1,0:T(8,128)(2,1)} async-done(((bf16[2560,2560]{1,0:T(8,128)(2,1)}), bf16[160,2560]{1,0:T(8,128)(2,1)}) %reduce-scatter.4.cloned.1.call-update) | async-done | bytes 819216 | tf_op jit(solution)/shard_map/reduce_scatter | solution.py:64
  341.5 6.0 %fusion.16 = (bf16[160,2560]{1,0:T(8,128)(2,1)}, f32[160,2560]{1,0:T(8,128)}, f32[1,160,2560]{2,1,0:T(8,128)}, f32[1,160,2560]{2,1,0:T(8,128)}) fusion(f32[1,160,2560]{2,1,0:T(8,128)} %param.11, bf16[160,2560]{1,0:T(8,128)(2,1)} %reduce-scatter.4.cloned.1.call-done, f32[1,160,2560]{2,1,0:T(8,128)} %param.10, f32[1,160,2560]{2,1,0:T(8,128)S(1)} %copy-done.2), kind=kLoop, calls=%fused_computation.34 | loop fusion | flops 6963200 | bytes 11468800 | tf_op jit(solution)/shard_map/convert_element_type | solution.py:81
  347.5 0.0 all-gather.5.cloned.1.call-update
  347.5 92.4 %all-gather.5.cloned.1.call-done = bf16[2560,2560]{1,0:T(8,128)(2,1)} async-done(((bf16[160,2560]{1,0:T(8,128)(2,1)}), bf16[2560,2560]{1,0:T(8,128)(2,1)}) %all-gather.5.cloned.1.call-update) | async-done | bytes 13107216 | tf_op jit(solution)/shard_map/all_gather | solution.py:85
  439.9 7.9 %fusion.2 = bf16[1,32,2560]{2,1,0:T(8,128)(2,1)} fusion(bf16[2560,2560]{1,0:T(8,128)(2,1)} %all-gather.5.cloned.1.call-done, bf16[1,32,2560]{2,1,0:T(8,128)(2,1)S(1)} %copy-done.5), kind=kOutput, calls=%fused_computation.6 | convolution fusion | flops 419512320 | bytes 13434880 | tf_op jit(solution)/shard_map/dot_general | solution.py:83
  (10 shorter events, 0.0 us)
Async XLA Ops:
  7.2 115.4 %copy-start = (bf16[1,4,128,2560]{3,2,1,0:T(8,128)(2,1)S(1)}, bf16[1,4,128,2560]{3,2,1,0:T(8,128)(2,1)}, u32[]{:S(2)}) copy-start(bf16[1,4,128,2560]{3,2,1,0:T(8,128)(2,1)} %param.12) | copy-start | bytes 7864324
  7.2 100.0 %all-gather.3.cloned.1.call-start = ((), (), s32[]{:S(2)}) async-start(), calls=%async_computation.1 | async-start | bytes 13926400 | tf_op jit(solution)/shard_map/all_gather | solution.py:49
  9.8 331.7 %reduce-scatter.4.cloned.1.call-start = ((), (), s32[]{:S(2)}) async-start(), calls=%async_computation.3 | async-start | bytes 13926400 | tf_op jit(solution)/shard_map/reduce_scatter | solution.py:64
  107.2 15.4 %copy-start.3 = (bf16[4,128,2560]{2,1,0:T(8,128)(2,1)S(1)}, bf16[4,128,2560]{2,1,0:T(8,128)(2,1)}, u32[]{:S(2)}) copy-start(bf16[4,128,2560]{2,1,0:T(8,128)(2,1)} %maximum_convert_fusion) | copy-start | bytes 7864324
  121.1 60.3 %collective-permute-start = (bf16[4,128,2560]{2,1,0:T(8,128)(2,1)}, bf16[4,128,2560]{2,1,0:T(8,128)(2,1)S(1)}, u32[]{:S(2)}, u32[]{:S(2)}) collective-permute-start(bf16[4,128,2560]{2,1,0:T(8,128)(2,1)} %bitcast.85), channel_id=1, source_target_pairs={{16,0},{32,16},{48,32},{64,48},{80,64},{96,80},{112,96},{17,1},{33... | collective-permute-start | bytes 7864328 | tf_op jit(solution)/shard_map/ppermute | solution.py:19
  122.6 58.8 %copy-start.4 = (s32[1,128,2560]{2,1,0:T(8,128)S(1)}, s32[1,128,2560]{2,1,0:T(8,128)}, u32[]{:S(2)}) copy-start(s32[1,128,2560]{2,1,0:T(8,128)} %param.16) | copy-start | bytes 3932164
  218.4 123.1 %copy-start.2 = (f32[1,160,2560]{2,1,0:T(8,128)S(1)}, f32[1,160,2560]{2,1,0:T(8,128)}, u32[]{:S(2)}) copy-start(f32[1,160,2560]{2,1,0:T(8,128)} %param.9) | copy-start | bytes 4915204
  218.5 221.5 %copy-start.5 = (bf16[1,32,2560]{2,1,0:T(8,128)(2,1)S(1)}, bf16[1,32,2560]{2,1,0:T(8,128)(2,1)}, u32[]{:S(2)}) copy-start(bf16[1,32,2560]{2,1,0:T(8,128)(2,1)} %param.17) | copy-start | bytes 491524
  218.5 221.5 %all-gather.5.cloned.1.call-start = ((), (), s32[]{:S(2)}) async-start(), calls=%async_computation.2 | async-start | bytes 13926400 | tf_op jit(solution)/shard_map/all_gather | solution.py:85
  439.9 7.9 %copy-start.1 = (bf16[1,4,128,2560]{3,2,1,0:T(8,128)(2,1)S(1)}, bf16[1,4,128,2560]{3,2,1,0:T(8,128)(2,1)}, u32[]{:S(2)}) copy-start(bf16[1,4,128,2560]{3,2,1,0:T(8,128)(2,1)} %param.12) | copy-start | bytes 7864324
Sparse Core Ops, SparseCore 0:
  11.0 96.1 all-gather.2
  218.6 122.9 reduce-scatter.3
  347.7 92.2 all-gather.4
where the time goes:
time: 455 us; the launch traced here: 454 us
  waiting for transfers between devices  354 us (78%)
  matrix products  50.5 us (11%)
  local copies, waits for them, and re-layouts  17.7 us (4%)
  other arithmetic  16.5 us (4%)
  between operations  13.8 us (3%)
    reduce_scatter x1, waiting for transfers between devices, shards(): lax.psum_scatter((partial_value + lax.dot_general(acts_arriving, membrane...  123 us
    all_gather x1, waiting for transfers between devices, shards(): lax.all_gather(fresh_weights, 'dp', axis=0, tiled=True)  92.4 us
    all_gather x1, waiting for transfers between devices, shards(): lax.all_gather(params.astype(jnp.bfloat16), 'dp', axis=0, tiled=True)  92.3 us
    ppermute x1, waiting for transfers between devices, passed_along(): return lax.ppermute(shard, axis, pairs)  46.4 us
    unnamed x13, local copies, waits for them, and re-layouts  17.7 us
    dot_general x1, matrix products, shards(): lax.dot_general(acts_arriving, membrane_arriving, contract, preferred_ele...  16.4 us
    dot_general x1, matrix products, shards(): lax.dot_general(membrane_own, lax.all_gather(params.astype(jnp.bfloat16),...  13.9 us
    dot_general x1, matrix products, shards(): lax.dot_general(acts_own, membrane_own, contract, preferred_element_type=...  12.3 us
  transfers between devices with their start and end apart: 4, of which 4 were waited for; matrix products, arithmetic and copies ran while one was open for 4% of the time, Pallas kernels for 0%

commit v1 on v0

v1 whole, which is shorter than its diff:
```python
import jax
import jax.numpy as jnp
from jax import lax
from jax.experimental import pallas as pl
from jax.experimental.pallas import tpu as pltpu
from jax.sharding import PartitionSpec as P

LEAK_RATE = 0.5
LEARN_RATE = 0.002
FIRST_DECAY = 0.9
SECOND_DECAY = 0.95
EPSILON = 1e-08
WEIGHT_DECAY = 0.1
FIRST_CORRECTION = 1.0 - 0.9**10
SECOND_CORRECTION = 1.0 - 0.95**10

MESH = pl.DeviceIdType.MESH
F32, BF16 = jnp.float32, jnp.bfloat16
FEAT, HALF, QUART, OWN = 2560, 1280, 640, 160
ROWS, TOK, STEPS = 512, 128, 4
YW = 768
XW = HALF - YW


def al(value, by):
    return pl.multiple_of(value, by)


def kernel(
    master, first, second, xo, xa, grads, wo, wa, ni,
    out_p, out_m, out_v, out_c,
    wb, mo, mos, xov, xav, acc, gv, wov, wav, mst, outb, rcv, niw,
    r1, r23, rx, qx, q1, q23, gx, cz, cr, res,
    loc, snd, wr, ws, xs, nr, pr, rr, zr, cs,
):
    s, d = lax.axis_index("section"), lax.axis_index("dp")
    y, xh, c, k = d // 4, (d // 2) % 2, d % 2, d // 2
    yp, ym, y2 = (y + 1) % 4, (y + 3) % 4, (y + 2) % 4

    def index(y_, xh_, c_):
        return (y_ * 2 + xh_) * 2 + c_

    sib, xp = (s, index(y, xh, 1 - c)), (s, index(y, 1 - xh, c))
    up, down = (s, index(yp, xh, c)), (s, index(ym, xh, c))
    used = [0]

    def send(src, dst, sem, dev):
        copy = pltpu.make_async_remote_copy(
            src_ref=src, dst_ref=dst, send_sem=snd.at[used[0]], recv_sem=sem,
            device_id=dev, device_id_type=MESH,
        )
        used[0] += 1
        copy.start()
        return copy

    def arrived(dst, sem):
        pltpu.make_async_remote_copy(
            src_ref=dst, dst_ref=dst, send_sem=snd.at[0], recv_sem=sem,
            device_id=sib, device_id_type=MESH,
        ).wait_recv()

    def load(src, dst, i):
        copy = pltpu.make_async_copy(src, dst, loc.at[i])
        copy.start()
        return copy

    def owner(y_, xh_, c_, part=0, rows=OWN):
        return wb.at[pl.ds(al(index(y_, xh_, c_) * OWN + part, 16), rows)]

    def half(which):
        return pl.ds(al(which * HALF, 128), HALF)

    l_mst = load(master, mst, 0)
    l_g = load(grads, gv, 1)
    l_wo = load(wo, wov, 2)
    l_xo = load(xo, xov.at[c], 3)
    l_xa = load(xa, xav.at[c], 4)
    l_wa = load(wa.at[:, half(c)], wav.at[c], 5)

    def base(e):
        return al(e * OWN - (e % 4) * 32, 128)

    l_ni = load(
        ni.at[:, pl.ds(base(d), 256)], niw.at[pl.ds(al(c * 256 + k * 32, 32), 32)], 6
    )

    barrier = pltpu.get_barrier_semaphore()
    for i in range(1, 16):
        pl.semaphore_signal(barrier, inc=1, device_id=(s, (d + i) % 16), device_id_type=MESH)

    @pl.when(s > 0)
    def _():
        for h in range(2):
            pl.semaphore_signal(barrier, inc=1, device_id=(s - 1, k * 2 + h), device_id_type=MESH)

    @pl.when(s < 7)
    def _():
        for h in range(2):
            pl.semaphore_signal(barrier, inc=1, device_id=(s + 1, k * 2 + h), device_id_type=MESH)

    l_mst.wait()

    @pl.loop(0, OWN // 16)
    def _(r):
        wb[pl.ds(al(d * OWN + r * 16, 16), 16), :] = mst[pl.ds(al(r * 16, 16), 16), :].astype(BF16)

    pl.semaphore_wait(barrier, 15 + 2 * jnp.minimum(s, 1) + 2 * jnp.minimum(7 - s, 1))

    mine = owner(y, xh, c)
    w_sends = [
        send(mine, mine, wr.at[0], xp),
        send(mine, mine, wr.at[1], up),
        send(mine, mine, wr.at[2], down),
        send(mine, mine, ws.at[0], sib),
    ]
    x_sends = [
        send(xo, xov.at[c], xs.at[0], sib),
        send(wa.at[:, half(1 - c)], wav.at[c], xs.at[1], sib),
        send(xa, xav.at[c], xs.at[2], sib),
    ]
    n_sends = []
    for i in range(1, 16):
        e = (d + i) % 16
        n_sends.append(
            send(
                ni.at[:, pl.ds(base(e), 256)],
                niw.at[pl.ds(al(c * 256 + k * 32, 32), 32)],
                nr.at[i],
                (s, e),
            )
        )

    l_g.wait()
    l_wo.wait()

    @pl.loop(0, TOK // 16)
    def _(r):
        for q in range(4):
            cols = pl.ds(q * QUART, QUART)
            bits = wov[pl.ds(al(r * 16, 16), 16), cols]
            carry = jnp.zeros((16, QUART), F32)
            for t in reversed(range(STEPS)):
                rows = pl.ds(al(t * TOK + r * 16, 16), 16)
                window = ((bits >> t) & 1).astype(F32)
                carry = window * gv[rows, cols].astype(F32) + LEAK_RATE * carry
                mo[rows, cols] = carry.astype(BF16)

    x_sends.append(send(mo.at[:, half(1 - c)], mos, xs.at[3], sib))

    across = (((0,), (0,)), ((), ()))
    l_xo.wait()
    arrived(xov.at[1 - c], xs.at[0])
    arrived(mos, xs.at[3])

    @pl.loop(0, 4)
    def _(b):
        rows = pl.ds(al(b * QUART, 128), QUART)
        for j in range(2):
            acc[rows, pl.ds(j * QUART, QUART)] = lax.dot_general(
                xov[c, :, rows],
                mo[:, pl.ds(al(c * HALF + j * QUART, 128), QUART)],
                across,
                preferred_element_type=F32,
            ) + lax.dot_general(
                xov[1 - c, :, rows],
                mos[:, pl.ds(j * QUART, QUART)],
                across,
                preferred_element_type=F32,
            )

    p_sends = []

    def outgoing(b, n):
        cols = pl.ds(al(b * QUART, 128), QUART)
        for h in (1, 0):
            rows = pl.ds(h * 256, 256)
            through = lax.dot_general(
                mo[rows, :], wb[cols, :], (((1,), (1,)), ((), ())), preferred_element_type=F32
            )
            outb[n, rows, :] = (gv[rows, cols].astype(F32) + through).astype(BF16)

            copy = pltpu.make_async_remote_copy(
                src_ref=outb.at[n, rows],
                dst_ref=rcv.at[c, b % 2, rows],
                send_sem=snd.at[used[0]],
                recv_sem=pr.at[c, b % 2, h],
                device_id=(s - 1, k * 2 + b // 2),
                device_id_type=MESH,
            )
            used[0] += 1
            p_sends.append(copy)
            pl.when(s > 0)(copy.start)

    def relay(kind, piece, *targets):
        arrived(piece, wr.at[kind])
        for region, sem, dev in targets:
            w_sends.append(send(region, region, sem, dev))

    piece = owner(y, 1 - xh, c)
    relay(0, piece, (piece, wr.at[3], up), (piece, wr.at[4], down), (piece, ws.at[1], sib))
    piece = owner(ym, xh, c)
    relay(1, piece, (owner(ym, xh, c, 0, 80), wr.at[5], up), (piece, ws.at[2], sib))
    piece = owner(yp, xh, c)
    relay(2, piece, (owner(yp, xh, c, 80, 80), wr.at[6], down), (piece, ws.at[3], sib))
    arrived(owner(y, xh, 1 - c), ws.at[0])
    arrived(owner(y, 1 - xh, 1 - c), ws.at[1])
    outgoing(y, 0)
    piece = owner(ym, 1 - xh, c)
    relay(3, piece, (owner(ym, 1 - xh, c, 0, 80), wr.at[7], up), (piece, ws.at[4], sib))
    piece = owner(yp, 1 - xh, c)
    relay(4, piece, (owner(yp, 1 - xh, c, 80, 80), wr.at[8], down), (piece, ws.at[5], sib))
    arrived(owner(ym, xh, 1 - c), ws.at[2])
    arrived(owner(ym, 1 - xh, 1 - c), ws.at[4])
    outgoing(ym, 1)
    arrived(owner(yp, xh, 1 - c), ws.at[3])
    arrived(owner(yp, 1 - xh, 1 - c), ws.at[5])
    outgoing(yp, 2)
    for i, (xh_, part) in enumerate(((xh, 0), (xh, 80), (1 - xh, 0), (1 - xh, 80))):
        piece = owner(y2, xh_, c, part, 80)
        relay(5 + i, piece, (piece, ws.at[6 + i], sib))
    for i, (xh_, part) in enumerate(((xh, 0), (xh, 80), (1 - xh, 0), (1 - xh, 80))):
        arrived(owner(y2, xh_, 1 - c, part, 80), ws.at[6 + i])
    outgoing(y2, 3)

    def far(b):
        away = (b - y + 4) % 4
        return jnp.minimum(away, 4 - away)

    early = jnp.where(far(2 * c) < far(2 * c + 1), 0, 1)
    late = 1 - early
    l_xa.wait()
    arrived(xav.at[1 - c], xs.at[2])
    l_wa.wait()
    arrived(wav.at[1 - c], xs.at[1])

    def arriving(j):
        for cc in range(2):
            for h in (1, 0):
                arrived(rcv.at[cc, j, pl.ds(h * 256, 256)], pr.at[cc, j, h])

            @pl.loop(0, TOK // 16)
            def _(r, cc=cc):
                bits = wav[cc, pl.ds(al(r * 16, 16), 16), pl.ds(al(j * QUART, 128), QUART)]
                carry = jnp.zeros((16, QUART), F32)
                for t in reversed(range(STEPS)):
                    rows = pl.ds(al(t * TOK + r * 16, 16), 16)
                    window = ((bits >> t) & 1).astype(F32)
                    carry = window * rcv[cc, j, rows, :].astype(F32) + LEAK_RATE * carry
                    rcv[cc, j, rows, :] = carry.astype(BF16)

    def more(b, j):
        rows = pl.ds(al(b * QUART, 128), QUART)
        cols = pl.ds(al(j * QUART, 128), QUART)
        acc[rows, cols] += lax.dot_general(
            xav[0, :, rows], rcv[0, j], across, preferred_element_type=F32
        ) + lax.dot_general(xav[1, :, rows], rcv[1, j], across, preferred_element_type=F32)

    @pl.when(s < 7)
    def _():
        arriving(early)

        @pl.loop(0, 4)
        def _(b):
            more(b, early)

        arriving(late)

    for copy in w_sends + x_sends:
        copy.wait_send()

    def unit(y_, xh_, n=2, first_=0):
        return pl.ds(al((y_ * 2 + xh_) * 2 * OWN + first_ * OWN, 32), n * OWN)

    def rounded(b):
        @pl.loop(0, QUART // 32)
        def _(r):
            rows = pl.ds(al(b * QUART + r * 32, 32), 32)
            wb[rows, pl.ds(0, HALF)] = acc[rows, :].astype(BF16)

    def finish(b):
        @pl.when(s < 7)
        def _():
            more(b, late)

        rounded(b)

    ycol, xcol = pl.ds(0, YW), pl.ds(YW, XW)
    r_sends = []

    def to_partner(b, n):
        r_sends.append(send(wb.at[unit(b, 1 - xh), xcol], qx.at[n], rr.at[7 + n], xp))

    finish(y2)
    r_sends.append(send(wb.at[unit(y2, 0), ycol], r1.at[0], rr.at[0], up))
    r_sends.append(send(wb.at[unit(y2, 1), ycol], r1.at[1], rr.at[1], down))
    to_partner(y2, 0)
    finish(yp)
    r_sends.append(send(wb.at[unit(yp, 1), ycol], r23.at[0, 1], rr.at[3], up))
    to_partner(yp, 1)
    finish(ym)
    r_sends.append(send(wb.at[unit(ym, 0), ycol], r23.at[1, 0], rr.at[4], down))
    to_partner(ym, 2)
    finish(y)
    to_partner(y, 3)

    def add(start, count, cols, *terms, to=None, keep=False):
        @pl.loop(0, count // 32)
        def _(r):
            rows = pl.ds(al(start + r * 32, 32), 32)
            total = acc[rows, cols]
            for term in terms:
                total += term[pl.ds(al(r * 32, 32), 32), :].astype(F32)
            if keep:
                acc[rows, cols] = total
            else:
                wb[rows, cols] = total.astype(BF16)

    def at_unit(y_, xh_, c_=0):
        return index(y_, xh_, c_) * OWN

    arrived(r1.at[0], rr.at[0])
    add(at_unit(yp, 0), 2 * OWN, ycol, r1.at[0])
    r_sends.append(send(wb.at[unit(yp, 0), ycol], r23.at[0, 0], rr.at[2], up))
    arrived(r1.at[1], rr.at[1])
    add(at_unit(ym, 1), 2 * OWN, ycol, r1.at[1])
    r_sends.append(send(wb.at[unit(ym, 1), ycol], r23.at[1, 1], rr.at[5], down))

    arrived(qx.at[0], rr.at[7])
    add(at_unit(y2, xh), 2 * OWN, xcol, qx.at[0])
    r_sends.append(send(wb.at[unit(y2, xh, 1, 0), xcol], q1.at[0], rr.at[11], up))
    r_sends.append(send(wb.at[unit(y2, xh, 1, 1), xcol], q1.at[1], rr.at[12], down))
    arrived(qx.at[1], rr.at[8])
    add(at_unit(yp, xh, 1), OWN, xcol, qx.at[1, pl.ds(OWN, OWN)])
    r_sends.append(send(wb.at[unit(yp, xh, 1, 1), xcol], q23.at[0, 1], rr.at[14], up))
    add(at_unit(yp, xh, 0), OWN, xcol, qx.at[1, pl.ds(0, OWN)], keep=True)
    arrived(qx.at[2], rr.at[9])
    add(at_unit(ym, xh, 0), OWN, xcol, qx.at[2, pl.ds(0, OWN)])
    r_sends.append(send(wb.at[unit(ym, xh, 1, 0), xcol], q23.at[1, 0], rr.at[15], down))
    add(at_unit(ym, xh, 1), OWN, xcol, qx.at[2, pl.ds(OWN, OWN)], keep=True)
    l_m = [load(first.at[:, half(h)], acc.at[unit(y2, h, 1, 0)], 7 + h) for h in range(2)]
    l_v = [load(second.at[:, half(h)], acc.at[unit(y2, h, 1, 1)], 9 + h) for h in range(2)]

    arrived(r23.at[0, 1], rr.at[3])
    arrived(r23.at[1, 0], rr.at[4])
    arrived(r23.at[0, 0], rr.at[2])
    arrived(r23.at[1, 1], rr.at[5])
    arrived(qx.at[3], rr.at[10])
    add(at_unit(y, 1 - xh), 2 * OWN, ycol, r23.at[0, 1 - xh], r23.at[1, 1 - xh])
    r_sends.append(send(wb.at[unit(y, 1 - xh), ycol], rx, rr.at[6], xp))
    add(at_unit(y, xh), 2 * OWN, ycol, r23.at[0, xh], r23.at[1, xh], keep=True)

    arrived(q1.at[0], rr.at[11])
    add(at_unit(yp, xh, 0), OWN, xcol, q1.at[0])
    r_sends.append(send(wb.at[unit(yp, xh, 1, 0), xcol], q23.at[0, 0], rr.at[13], up))
    arrived(q1.at[1], rr.at[12])
    add(at_unit(ym, xh, 1), OWN, xcol, q1.at[1])
    r_sends.append(send(wb.at[unit(ym, xh, 1, 1), xcol], q23.at[1, 1], rr.at[16], down))
    for u in range(2):
        arrived(q23.at[0, 1 - u], rr.at[13 + (1 - u)])
        arrived(q23.at[1, u], rr.at[15 + u])
    for u in range(2):
        add(
            at_unit(y, xh, u), OWN, xcol,
            qx.at[3, pl.ds(u * OWN, OWN)], q23.at[0, u], q23.at[1, u], keep=True,
        )
    arrived(rx, rr.at[6])
    add(at_unit(y, xh), 2 * OWN, ycol, rx, keep=True)

    r_sends.append(send(acc.at[pl.ds(al(at_unit(y, xh, 1 - c), 32), OWN)], gx, rr.at[17], sib))

    @pl.loop(0, 256 // 32)
    def _(r):
        mo[pl.ds(al(r * 32, 32), 32), :] = jnp.zeros((32, FEAT), BF16)

    for copy in l_m + l_v:
        copy.wait()
    shift = (d % 4) * 32
    stores = []

    def adam(which, gradient, start):
        @pl.loop(0, OWN // 16)
        def _(r):
            here = pl.ds(al(r * 16, 16), 16)
            cols = half(which)
            at_m = pl.ds(al(at_unit(y2, which, 0) + r * 16, 16), 16)
            at_v = pl.ds(al(at_unit(y2, which, 1) + r * 16, 16), 16)
            g = gradient[pl.ds(al(start + r * 16, 16), 16), :]
            params = mst[here, cols]
            m = FIRST_DECAY * acc[at_m, :] + (1.0 - FIRST_DECAY) * g
            v = SECOND_DECAY * acc[at_v, :] + (1.0 - SECOND_DECAY) * g * g
            acc[at_m, :] = m
            acc[at_v, :] = v
            direction = m / FIRST_CORRECTION / (jnp.sqrt(v / SECOND_CORRECTION) + EPSILON)
            new = params - LEARN_RATE * (direction + WEIGHT_DECAY * params)
            mst[here, cols] = new
            mo[pl.ds(al(shift + r * 16, 16), 16), cols] = new.astype(BF16)

        n = 11 if which is c else 14
        stores.append(load(mst.at[:, half(which)], out_p.at[:, half(which)], n))
        stores.append(load(acc.at[unit(y2, which, 1, 0)], out_m.at[:, half(which)], n + 1))
        stores.append(load(acc.at[unit(y2, which, 1, 1)], out_v.at[:, half(which)], n + 2))

    adam(c, acc, at_unit(y, xh, c))
    arrived(gx, rr.at[17])
    adam(1 - c, gx, 0)

    l_ni.wait()
    for i in range(1, 16):
        e = (d - i + 16) % 16
        arrived(niw.at[pl.ds(al((e % 2) * 256 + (e // 2) * 32, 32), 32)], nr.at[i])
    c_sends = []
    for q in range(4):
        cols = pl.ds(q * QUART, QUART)
        gv[pl.ds(0, 256), cols] = jnp.dot(
            niw[pl.ds(al((1 - c) * 256, 256), 256), :],
            mo[pl.ds(0, 256), cols],
            preferred_element_type=F32,
        ).astype(BF16)
        c_sends.append(send(gv.at[pl.ds(0, 256), cols], cz.at[:, cols], zr.at[q], sib))
    for q in range(4):
        cols = pl.ds(q * QUART, QUART)
        total = jnp.dot(
            niw[pl.ds(al(c * 256, 256), 256), :],
            mo[pl.ds(0, 256), cols],
            preferred_element_type=F32,
        )
        arrived(cz.at[:, cols], zr.at[q])
        gv[pl.ds(256, 256), cols] = (total + cz[:, cols].astype(F32)).astype(BF16)
    for i in range(1, 8):
        e = (k + i) % 8
        c_sends.append(
            send(
                gv.at[pl.ds(al(256 + e * 32, 32), 32)],
                cr.at[i],
                cs.at[i],
                (s, e * 2 + c),
            )
        )
    for i in range(1, 8):
        arrived(cr.at[i], cs.at[i])

    @pl.loop(0, 2)
    def _(r):
        here = pl.ds(al(r * 16, 16), 16)
        for q in range(4):
            cols = pl.ds(q * QUART, QUART)
            total = gv[pl.ds(al(256 + k * 32 + r * 16, 16), 16), cols].astype(F32)
            for i in range(1, 8):
                total += cr[i, here, cols].astype(F32)
            res[here, cols] = total.astype(BF16)

    stores.append(load(res, out_c, 17))
    for copy in stores:
        copy.wait()
    for copy in n_sends + r_sends + c_sends:
        copy.wait_send()

    @pl.when(s > 0)
    def _():
        for copy in p_sends:
            copy.wait_send()


def step(master, first, second, xo, xa, grads, wo, wa, ni):
    vm = pltpu.VMEM
    dma = pltpu.SemaphoreType.DMA
    anywhere = pl.BlockSpec(memory_space=pl.ANY)
    shape = jax.ShapeDtypeStruct
    flat = (ROWS, FEAT)
    new = pl.pallas_call(
        kernel,
        out_shape=(
            shape((OWN, FEAT), F32),
            shape((OWN, FEAT), F32),
            shape((OWN, FEAT), F32),
            shape((32, FEAT), BF16),
        ),
        in_specs=[anywhere] * 9,
        out_specs=[anywhere] * 4,
        scratch_shapes=[
            vm((FEAT, FEAT), BF16),
            vm(flat, BF16),
            vm((ROWS, HALF), BF16),
            vm((2, ROWS, FEAT), BF16),
            vm((2, ROWS, FEAT), BF16),
            vm((FEAT, HALF), F32),
            vm(flat, BF16),
            vm((TOK, FEAT), jnp.int32),
            vm((2, TOK, HALF), jnp.int32),
            vm((OWN, FEAT), F32),
            vm((4, ROWS, QUART), BF16),
            vm((2, 2, ROWS, QUART), BF16),
            vm((512, 256), BF16),
            vm((2, 2 * OWN, YW), BF16),
            vm((2, 2, 2 * OWN, YW), BF16),
            vm((2 * OWN, YW), BF16),
            vm((4, 2 * OWN, XW), BF16),
            vm((2, OWN, XW), BF16),
            vm((2, 2, OWN, XW), BF16),
            vm((OWN, HALF), F32),
            vm((256, FEAT), BF16),
            vm((8, 32, FEAT), BF16),
            vm((32, FEAT), BF16),
            dma((18,)),
            dma((96,)),
            dma((9,)),
            dma((10,)),
            dma((4,)),
            dma((16,)),
            dma((2, 2, 2)),
            dma((18,)),
            dma((4,)),
            dma((8,)),
        ],
        compiler_params=pltpu.CompilerParams(
            collective_id=0, has_side_effects=True, vmem_limit_bytes=67043328
        ),
        name="section_step",
    )(
        master[0],
        first[0],
        second[0],
        xo[0].reshape(flat),
        xa[0].reshape(flat),
        grads[0].reshape(flat),
        wo[0],
        wa[0],
        ni[0],
    )
    return tuple(value[None] for value in new)


def solution(mesh):
    row = P("section", "dp", None)
    deep = P("section", None, "dp", None)
    return jax.shard_map(
        step,
        mesh=mesh,
        in_specs=(row, row, row, deep, deep, deep, row, row, row),
        out_specs=(row, row, row, row),
        check_vma=False,
    )
```

time: 455 us -> 170 us (0.37)
  waiting for transfers between devices: 354 us -> 0 us
  Pallas kernels: 0 us -> 162 us
  matrix products: 50.5 us -> 0 us
  other arithmetic: 16.5 us -> 0 us
  between operations: 13.8 us -> 0.65 us
  local copies, waits for them, and re-layouts: 17.7 us -> 6.69 us
    all_gather x2 -> x0, waiting for transfers between devices: 185 us -> none  [the longest x1 92.4 us: shards(): lax.all_gather(fresh_weights, 'dp', axis=0, tiled=True)]
    pallas_call x0 -> x1, Pallas kernels: none -> 162 us  [step(): pl.pallas_call(kernel, out_shape=(shape((OWN, FEAT), F32), shape((OWN, FE...]
    reduce_scatter x1 -> x0, waiting for transfers between devices: 123 us -> none  [shards(): lax.psum_scatter((partial_value + lax.dot_general(acts_arriving, membrane...]
    dot_general x4 -> x0, matrix products: 50.5 us -> none  [the longest x1 16.4 us: shards(): lax.dot_general(acts_arriving, membrane_arriving, contract, preferred_ele...]
    ppermute x1 -> x0, waiting for transfers between devices: 46.4 us -> none  [passed_along(): return lax.ppermute(shard, axis, pairs)]
    unnamed x13 -> x10, local copies, waits for them, and re-layouts: 17.7 us -> 6.69 us
    convert_element_type x3 -> x0, other arithmetic: 10.3 us -> none  [the longest x1 5.98 us: shards(): fresh_weights = fresh_params.astype(jnp.bfloat16)]
  transfers between devices with their start and end apart: 4 -> 0, of which waited for: 4 -> 0; matrix products, arithmetic and copies ran while one was open for 4% -> 0% of each run, Pallas kernels for 0% -> 0%
where the time goes in v1:
time: 170 us; the launch traced here: 169 us
  Pallas kernels  162 us (95%)
  local copies, waits for them, and re-layouts  6.69 us (4%)
    pallas_call x1, Pallas kernels, step(): pl.pallas_call(kernel, out_shape=(shape((OWN, FEAT), F32), shape((OWN, FE...  162 us
    unnamed x10, local copies, waits for them, and re-layouts  6.69 us

profile of v1, /device:TPU:1, one launch (start us, length us, event | category | flops | bytes accessed | tf_op | source)
XLA Modules:
  0.0 169.0 jit_solution(10397763291104249152)
XLA Ops:
  0.6 161.7 %section_step.1 = (f32[160,2560]{1,0:T(8,128)}, f32[160,2560]{1,0:T(8,128)}, f32[160,2560]{1,0:T(8,128)}, bf16[32,2560]{1,0:T(8,128)(2,1)}) custom-call(f32[160,2560]{1,0:T(8,128)} %bitcast.19, f32[160,2560]{1,0:T(8,128)} %bitcast.20, f32[160,2560]{1,0:T(8,128)} %bitcast.21, bf16[512,2560]{1,0:T(8,128)(2,1)} %bitcast.13, bf16[512,2560]{1,0:T(8,128)(2,1)} %bitcast.14, ...), custom_call_target="tpu_custom_call" | custom-call | tf_op jit(solution)/shard_map/section_step/pallas_call | solution.py:470
  162.3 0.0 copy-start.1
  162.3 2.8 %copy.17 = f32[1,160,2560]{2,1,0:T(8,128)} copy(f32[1,160,2560]{2,1,0:T(8,128)} %bitcast.18) | data formatting | bytes 3276800
  165.2 0.0 copy-done.1
  165.2 0.0 copy-start
  165.2 1.2 copy.18
  166.3 0.9 copy-done
  167.2 0.0 copy-start.2
  167.2 1.2 copy.19
  168.4 0.0 copy-done.2
  168.4 0.7 copy.20
Async XLA Ops:
  162.3 2.8 %copy-start.1 = (f32[160,2560]{1,0:T(8,128)S(1)}, f32[160,2560]{1,0:T(8,128)}, u32[]{:S(2)}) copy-start(f32[160,2560]{1,0:T(8,128)} %get-tuple-element.9) | copy-start | bytes 4915204
  165.2 2.0 %copy-start = (f32[160,2560]{1,0:T(8,128)S(1)}, f32[160,2560]{1,0:T(8,128)}, u32[]{:S(2)}) copy-start(f32[160,2560]{1,0:T(8,128)} %get-tuple-element.10) | copy-start | bytes 4915204
  167.2 1.2 copy-start.2

commit v2 on v1

--- a/solution.py
+++ b/solution.py
@@ -116,20 +116,7 @@
     x_sends = [
         send(xo, xov.at[c], xs.at[0], sib),
         send(wa.at[:, half(1 - c)], wav.at[c], xs.at[1], sib),
-        send(xa, xav.at[c], xs.at[2], sib),
     ]
-    n_sends = []
-    for i in range(1, 16):
-        e = (d + i) % 16
-        n_sends.append(
-            send(
-                ni.at[:, pl.ds(base(e), 256)],
-                niw.at[pl.ds(al(c * 256 + k * 32, 32), 32)],
-                nr.at[i],
-                (s, e),
-            )
-        )
-
     l_g.wait()
     l_wo.wait()
 
@@ -146,6 +133,53 @@
                 mo[rows, cols] = carry.astype(BF16)
 
     x_sends.append(send(mo.at[:, half(1 - c)], mos, xs.at[3], sib))
+    x_sends.append(send(xa, xav.at[c], xs.at[2], sib))
+
+    p_sends = []
+
+    parts = ((xh * 384, 256), ((1 - xh) * 256, 384))
+
+    def outgoing(b, n, part):
+        begin, width = parts[part]
+        cols = pl.ds(al(begin, 128), width)
+        wide = pl.ds(al(b * QUART + begin, 128), width)
+        for h in (1, 0):
+            rows = pl.ds(h * 256, 256)
+            through = lax.dot_general(
+                mo[rows, :], wb[wide, :], (((1,), (1,)), ((), ())), preferred_element_type=F32
+            )
+            outb[n, rows, cols] = (gv[rows, wide].astype(F32) + through).astype(BF16)
+            copy = pltpu.make_async_remote_copy(
+                src_ref=outb.at[n, rows, cols],
+                dst_ref=rcv.at[c, b % 2, rows, cols],
+                send_sem=snd.at[used[0]],
+                recv_sem=pr.at[c, b % 2, part, h],
+                device_id=(s - 1, k * 2 + b // 2),
+                device_id_type=MESH,
+            )
+            used[0] += 1
+            p_sends.append(copy)
+            pl.when(s > 0)(copy.start)
+
+    def relay(kind, piece, *targets):
+        arrived(piece, wr.at[kind])
+        for region, sem, dev in targets:
+            w_sends.append(send(region, region, sem, dev))
+
+    arrived(owner(y, xh, 1 - c), ws.at[0])
+    outgoing(y, 0, 0)
+    piece = owner(y, 1 - xh, c)
+    relay(0, piece, (piece, wr.at[3], up), (piece, wr.at[4], down), (piece, ws.at[1], sib))
+    piece = owner(ym, xh, c)
+    relay(1, piece, (owner(ym, xh, c, 0, 80), wr.at[5], up), (piece, ws.at[2], sib))
+    piece = owner(yp, xh, c)
+    relay(2, piece, (owner(yp, xh, c, 80, 80), wr.at[6], down), (piece, ws.at[3], sib))
+    arrived(owner(y, 1 - xh, 1 - c), ws.at[1])
+    outgoing(y, 0, 1)
+    arrived(owner(ym, xh, 1 - c), ws.at[2])
+    outgoing(ym, 1, 0)
+    arrived(owner(yp, xh, 1 - c), ws.at[3])
+    outgoing(yp, 2, 0)
 
     across = (((0,), (0,)), ((), ()))
     l_xo.wait()
@@ -168,59 +202,21 @@
                 preferred_element_type=F32,
             )
 
-    p_sends = []
-
-    def outgoing(b, n):
-        cols = pl.ds(al(b * QUART, 128), QUART)
-        for h in (1, 0):
-            rows = pl.ds(h * 256, 256)
-            through = lax.dot_general(
-                mo[rows, :], wb[cols, :], (((1,), (1,)), ((), ())), preferred_element_type=F32
-            )
-            outb[n, rows, :] = (gv[rows, cols].astype(F32) + through).astype(BF16)
-
-            copy = pltpu.make_async_remote_copy(
-                src_ref=outb.at[n, rows],
-                dst_ref=rcv.at[c, b % 2, rows],
-                send_sem=snd.at[used[0]],
-                recv_sem=pr.at[c, b % 2, h],
-                device_id=(s - 1, k * 2 + b // 2),
-                device_id_type=MESH,
-            )
-            used[0] += 1
-            p_sends.append(copy)
-            pl.when(s > 0)(copy.start)
-
-    def relay(kind, piece, *targets):
-        arrived(piece, wr.at[kind])
-        for region, sem, dev in targets:
-            w_sends.append(send(region, region, sem, dev))
-
-    piece = owner(y, 1 - xh, c)
-    relay(0, piece, (piece, wr.at[3], up), (piece, wr.at[4], down), (piece, ws.at[1], sib))
-    piece = owner(ym, xh, c)
-    relay(1, piece, (owner(ym, xh, c, 0, 80), wr.at[5], up), (piece, ws.at[2], sib))
-    piece = owner(yp, xh, c)
-    relay(2, piece, (owner(yp, xh, c, 80, 80), wr.at[6], down), (piece, ws.at[3], sib))
-    arrived(owner(y, xh, 1 - c), ws.at[0])
-    arrived(owner(y, 1 - xh, 1 - c), ws.at[1])
-    outgoing(y, 0)
     piece = owner(ym, 1 - xh, c)
     relay(3, piece, (owner(ym, 1 - xh, c, 0, 80), wr.at[7], up), (piece, ws.at[4], sib))
     piece = owner(yp, 1 - xh, c)
     relay(4, piece, (owner(yp, 1 - xh, c, 80, 80), wr.at[8], down), (piece, ws.at[5], sib))
-    arrived(owner(ym, xh, 1 - c), ws.at[2])
     arrived(owner(ym, 1 - xh, 1 - c), ws.at[4])
-    outgoing(ym, 1)
-    arrived(owner(yp, xh, 1 - c), ws.at[3])
+    outgoing(ym, 1, 1)
     arrived(owner(yp, 1 - xh, 1 - c), ws.at[5])
-    outgoing(yp, 2)
-    for i, (xh_, part) in enumerate(((xh, 0), (xh, 80), (1 - xh, 0), (1 - xh, 80))):
-        piece = owner(y2, xh_, c, part, 80)
-        relay(5 + i, piece, (piece, ws.at[6 + i], sib))
-    for i, (xh_, part) in enumerate(((xh, 0), (xh, 80), (1 - xh, 0), (1 - xh, 80))):
-        arrived(owner(y2, xh_, 1 - c, part, 80), ws.at[6 + i])
-    outgoing(y2, 3)
+    outgoing(yp, 2, 1)
+    for n, xh_ in enumerate((xh, 1 - xh)):
+        for i in range(2):
+            piece = owner(y2, xh_, c, 80 * i, 80)
+            relay(5 + 2 * n + i, piece, (piece, ws.at[6 + 2 * n + i], sib))
+        for i in range(2):
+            arrived(owner(y2, xh_, 1 - c, 80 * i, 80), ws.at[6 + 2 * n + i])
+        outgoing(y2, 3, n)
 
     def far(b):
         away = (b - y + 4) % 4
@@ -235,8 +231,12 @@
 
     def arriving(j):
         for cc in range(2):
-            for h in (1, 0):
-                arrived(rcv.at[cc, j, pl.ds(h * 256, 256)], pr.at[cc, j, h])
+            for part, (begin, width) in enumerate(parts):
+                for h in (1, 0):
+                    arrived(
+                        rcv.at[cc, j, pl.ds(h * 256, 256), pl.ds(al(begin, 128), width)],
+                        pr.at[cc, j, part, h],
+                    )
 
             @pl.loop(0, TOK // 16)
             def _(r, cc=cc):
@@ -302,6 +302,18 @@
     to_partner(ym, 2)
     finish(y)
     to_partner(y, 3)
+    n_sends = []
+    for i in range(1, 16):
+        e = (d + i) % 16
+        n_sends.append(
+            send(
+                ni.at[:, pl.ds(base(e), 256)],
+                niw.at[pl.ds(al(c * 256 + k * 32, 32), 32)],
+                nr.at[i],
+                (s, e),
+            )
+        )
+
 
     def add(start, count, cols, *terms, to=None, keep=False):
         @pl.loop(0, count // 32)
@@ -459,6 +471,33 @@
     def _():
         for copy in p_sends:
             copy.wait_send()
+
+
+def settle_kernel(*refs):
+    count = len(refs) // 4
+    sources, targets, held, sems = (refs[i * count : (i + 1) * count] for i in range(4))
+    taken = [pltpu.make_async_copy(a, v, m.at[0]) for a, v, m in zip(sources, held, sems)]
+    given = [pltpu.make_async_copy(v, b, m.at[1]) for v, b, m in zip(held, targets, sems)]
+    for copy in taken:
+        copy.start()
+    for copy, onward in zip(taken, given):
+        copy.wait()
+        onward.start()
+    for copy in given:
+        copy.wait()
+
+
+def settle(*values):
+    anywhere = pl.BlockSpec(memory_space=pl.ANY)
+    return pl.pallas_call(
+        settle_kernel,
+        out_shape=tuple(jax.ShapeDtypeStruct(v.shape, v.dtype) for v in values),
+        in_specs=[anywhere] * len(values),
+        out_specs=[anywhere] * len(values),
+        scratch_shapes=[pltpu.VMEM(v.shape, v.dtype) for v in values]
+        + [pltpu.SemaphoreType.DMA((2,)) for _ in values],
+        name="settle",
+    )(*values)
 
 
 def step(master, first, second, xo, xa, grads, wo, wa, ni):
@@ -502,12 +541,12 @@
             vm((8, 32, FEAT), BF16),
             vm((32, FEAT), BF16),
             dma((18,)),
-            dma((96,)),
+            dma((112,)),
             dma((9,)),
             dma((10,)),
             dma((4,)),
             dma((16,)),
-            dma((2, 2, 2)),
+            dma((2, 2, 2, 2)),
             dma((18,)),
             dma((4,)),
             dma((8,)),
@@ -527,7 +566,7 @@
         wa[0],
         ni[0],
     )
-    return tuple(value[None] for value in new)
+    return tuple(value[None] for value in settle(*new))
 
 
 def solution(mesh):

time: 170 us -> 159 us (0.935)
  local copies, waits for them, and re-layouts: 6.69 us -> 0 us
  Pallas kernels: 162 us -> 158 us
    pallas_call x1, Pallas kernels: 162 us -> 154 us  [step(): pl.pallas_call(kernel, out_shape=(shape((OWN, FEAT), F32), shape((OWN, FE...]
    unnamed x10 -> x0, local copies, waits for them, and re-layouts: 6.69 us -> none
    pallas_call x0 -> x1, Pallas kernels: none -> 3.79 us  [settle(): pl.pallas_call(settle_kernel, out_shape=tuple((jax.ShapeDtypeStruct(v.sha...]
where the time goes in v2:
time: 159 us; the launch traced here: 158 us
  Pallas kernels  158 us (99%)
    pallas_call x1, Pallas kernels, step(): pl.pallas_call(kernel, out_shape=(shape((OWN, FEAT), F32), shape((OWN, FE...  154 us
    pallas_call x1, Pallas kernels, settle(): pl.pallas_call(settle_kernel, out_shape=tuple((jax.ShapeDtypeStruct(v.sha...  3.79 us

profile of v2, /device:TPU:1, one launch (start us, length us, event | category | flops | bytes accessed | tf_op | source)
XLA Modules:
  0.0 158.4 jit_solution(6539663801325250278)
XLA Ops:
  0.6 153.8 %section_step.1 = (f32[160,2560]{1,0:T(8,128)}, f32[160,2560]{1,0:T(8,128)}, f32[160,2560]{1,0:T(8,128)}, bf16[32,2560]{1,0:T(8,128)(2,1)}) custom-call(f32[160,2560]{1,0:T(8,128)} %bitcast.16, f32[160,2560]{1,0:T(8,128)} %bitcast.17, f32[160,2560]{1,0:T(8,128)} %bitcast.18, bf16[512,2560]{1,0:T(8,128)(2,1)} %bitcast.13, bf16[512,2560]{1,0:T(8,128)(2,1)} %bitcast.14, ...), custom_call_target="tpu_custom_call" | custom-call | tf_op jit(solution)/shard_map/section_step/pallas_call | solution.py:509
  154.5 3.8 %settle.1 = (f32[160,2560]{1,0:T(8,128)}, f32[160,2560]{1,0:T(8,128)}, f32[160,2560]{1,0:T(8,128)}, bf16[32,2560]{1,0:T(8,128)(2,1)}) custom-call(f32[160,2560]{1,0:T(8,128)} %get-tuple-element.12.refs_0_, f32[160,2560]{1,0:T(8,128)} %get-tuple-element.13.refs_1_, f32[160,2560]{1,0:T(8,128)} %get-tuple-element.14.refs_2_, ...), custom_call_target="tpu_custom_call" | custom-call | tf_op jit(solution)/shard_map/settle/pallas_call | solution.py:492

commit v3 on v2

--- a/solution.py
+++ b/solution.py
@@ -18,8 +18,8 @@
 F32, BF16 = jnp.float32, jnp.bfloat16
 FEAT, HALF, QUART, OWN = 2560, 1280, 640, 160
 ROWS, TOK, STEPS = 512, 128, 4
-YW = 768
-XW = HALF - YW
+PART, MID = 256, 128
+PAIR, MIDS = 2 * PART, 2 * MID
 
 
 def al(value, by):
@@ -30,7 +30,7 @@
     master, first, second, xo, xa, grads, wo, wa, ni,
     out_p, out_m, out_v, out_c,
     wb, mo, mos, xov, xav, acc, gv, wov, wav, mst, outb, rcv, niw,
-    r1, r23, rx, qx, q1, q23, gx, cz, cr, res,
+    n1, n23, r1, r23, rx, qx, q1, q23, gx, cz, cr, res,
     loc, snd, wr, ws, xs, nr, pr, rr, zr, cs,
 ):
     s, d = lax.axis_index("section"), lax.axis_index("dp")
@@ -168,12 +168,12 @@
 
     arrived(owner(y, xh, 1 - c), ws.at[0])
     outgoing(y, 0, 0)
-    piece = owner(y, 1 - xh, c)
-    relay(0, piece, (piece, wr.at[3], up), (piece, wr.at[4], down), (piece, ws.at[1], sib))
     piece = owner(ym, xh, c)
     relay(1, piece, (owner(ym, xh, c, 0, 80), wr.at[5], up), (piece, ws.at[2], sib))
     piece = owner(yp, xh, c)
     relay(2, piece, (owner(yp, xh, c, 80, 80), wr.at[6], down), (piece, ws.at[3], sib))
+    piece = owner(y, 1 - xh, c)
+    relay(0, piece, (piece, wr.at[3], up), (piece, wr.at[4], down), (piece, ws.at[1], sib))
     arrived(owner(y, 1 - xh, 1 - c), ws.at[1])
     outgoing(y, 0, 1)
     arrived(owner(ym, xh, 1 - c), ws.at[2])
@@ -202,6 +202,15 @@
                 preferred_element_type=F32,
             )
 
+    def far_block(xh_, n):
+        for i in range(2):
+            piece = owner(y2, xh_, c, 80 * i, 80)
+            relay(5 + 2 * n + i, piece, (piece, ws.at[6 + 2 * n + i], sib))
+        for i in range(2):
+            arrived(owner(y2, xh_, 1 - c, 80 * i, 80), ws.at[6 + 2 * n + i])
+        outgoing(y2, 3, n)
+
+    far_block(xh, 0)
     piece = owner(ym, 1 - xh, c)
     relay(3, piece, (owner(ym, 1 - xh, c, 0, 80), wr.at[7], up), (piece, ws.at[4], sib))
     piece = owner(yp, 1 - xh, c)
@@ -210,98 +219,140 @@
     outgoing(ym, 1, 1)
     arrived(owner(yp, 1 - xh, 1 - c), ws.at[5])
     outgoing(yp, 2, 1)
-    for n, xh_ in enumerate((xh, 1 - xh)):
-        for i in range(2):
-            piece = owner(y2, xh_, c, 80 * i, 80)
-            relay(5 + 2 * n + i, piece, (piece, ws.at[6 + 2 * n + i], sib))
-        for i in range(2):
-            arrived(owner(y2, xh_, 1 - c, 80 * i, 80), ws.at[6 + 2 * n + i])
-        outgoing(y2, 3, n)
-
-    def far(b):
-        away = (b - y + 4) % 4
-        return jnp.minimum(away, 4 - away)
-
-    early = jnp.where(far(2 * c) < far(2 * c + 1), 0, 1)
-    late = 1 - early
+
     l_xa.wait()
     arrived(xav.at[1 - c], xs.at[2])
     l_wa.wait()
     arrived(wav.at[1 - c], xs.at[1])
 
-    def arriving(j):
-        for cc in range(2):
-            for part, (begin, width) in enumerate(parts):
+    def arriving(part):
+        begin, width = parts[part]
+        cols = pl.ds(al(begin, 128), width)
+        for j in range(2):
+            for cc in range(2):
                 for h in (1, 0):
-                    arrived(
-                        rcv.at[cc, j, pl.ds(h * 256, 256), pl.ds(al(begin, 128), width)],
-                        pr.at[cc, j, part, h],
-                    )
-
-            @pl.loop(0, TOK // 16)
-            def _(r, cc=cc):
-                bits = wav[cc, pl.ds(al(r * 16, 16), 16), pl.ds(al(j * QUART, 128), QUART)]
-                carry = jnp.zeros((16, QUART), F32)
-                for t in reversed(range(STEPS)):
-                    rows = pl.ds(al(t * TOK + r * 16, 16), 16)
-                    window = ((bits >> t) & 1).astype(F32)
-                    carry = window * rcv[cc, j, rows, :].astype(F32) + LEAK_RATE * carry
-                    rcv[cc, j, rows, :] = carry.astype(BF16)
-
-    def more(b, j):
+                    arrived(rcv.at[cc, j, pl.ds(h * 256, 256), cols], pr.at[cc, j, part, h])
+
+                @pl.loop(0, TOK // 16)
+                def _(r, cc=cc, j=j):
+                    here = pl.ds(al(r * 16, 16), 16)
+                    bits = wav[cc, here, pl.ds(al(j * QUART + begin, 128), width)]
+                    carry = jnp.zeros((16, width), F32)
+                    for t in reversed(range(STEPS)):
+                        rows = pl.ds(al(t * TOK + r * 16, 16), 16)
+                        window = ((bits >> t) & 1).astype(F32)
+                        carry = window * rcv[cc, j, rows, cols].astype(F32) + LEAK_RATE * carry
+                        rcv[cc, j, rows, cols] = carry.astype(BF16)
+
+    def more(b, part):
+        begin, width = parts[part]
         rows = pl.ds(al(b * QUART, 128), QUART)
-        cols = pl.ds(al(j * QUART, 128), QUART)
-        acc[rows, cols] += lax.dot_general(
-            xav[0, :, rows], rcv[0, j], across, preferred_element_type=F32
-        ) + lax.dot_general(xav[1, :, rows], rcv[1, j], across, preferred_element_type=F32)
-
-    @pl.when(s < 7)
-    def _():
-        arriving(early)
-
-        @pl.loop(0, 4)
-        def _(b):
-            more(b, early)
-
-        arriving(late)
-
+        cols = pl.ds(al(begin, 128), width)
+
+        @pl.when(s < 7)
+        def _():
+            for j in range(2):
+                acc[rows, pl.ds(al(j * QUART + begin, 128), width)] += lax.dot_general(
+                    xav[0, :, rows], rcv[0, j, :, cols], across, preferred_element_type=F32
+                ) + lax.dot_general(
+                    xav[1, :, rows], rcv[1, j, :, cols], across, preferred_element_type=F32
+                )
+
+    near, rest, mid = (xh * 384, PART), ((1 - xh) * 384, PART), (PART, MID)
+    r_sends = []
+
+    def at_unit(y_, xh_, c_=0):
+        return index(y_, xh_, c_) * OWN
+
+    def unit(y_, xh_, n=2, first_=0):
+        return pl.ds(al(at_unit(y_, xh_, first_), 32), n * OWN)
+
+    def add(start, count, group, *terms, to=None):
+        begin, width = group
+        height = 32
+
+        @pl.loop(0, count // height)
+        def _(r):
+            rows = pl.ds(al(start + r * height, 32), height)
+            here = pl.ds(al(r * height, 32), height)
+            for j in range(2):
+                cols = pl.ds(al(j * QUART + begin, 128), width)
+                side = pl.ds(j * width, width)
+                total = acc[rows, cols]
+                for term in terms:
+                    total += term[here, side].astype(F32)
+                if to is None:
+                    acc[rows, cols] = total
+                else:
+                    to[here, side] = total.astype(BF16)
+
+    def pass_on(src, dst, sem, dev):
+        r_sends.append(send(src, dst, sem, dev))
+
+    class AlongY:
+        def __init__(self, group, place, one, two, sems):
+            self.group, self.place, self.one, self.two, self.sems = group, place, one, two, sems
+
+        def begin(self, b):
+            for xh_ in range(2):
+                keep = (b is yp and xh_ == 0) or (b is ym and xh_ == 1) or b is y
+                if keep:
+                    continue
+                ref = self.place(b, xh_)
+                add(at_unit(b, xh_), 2 * OWN, self.group, to=ref)
+                if b is y2:
+                    pass_on(ref, self.one.at[xh_], rr.at[self.sems + xh_], (up, down)[xh_])
+                elif b is yp:
+                    pass_on(ref, self.two.at[0, 1], rr.at[self.sems + 3], up)
+                else:
+                    pass_on(ref, self.two.at[1, 0], rr.at[self.sems + 4], down)
+
+        def middle(self):
+            for xh_, b, dev, sem in ((0, yp, up, 2), (1, ym, down, 5)):
+                arrived(self.one.at[xh_], rr.at[self.sems + xh_])
+                ref = self.place(b, xh_)
+                add(at_unit(b, xh_), 2 * OWN, self.group, self.one.at[xh_], to=ref)
+                pass_on(ref, self.two.at[xh_, xh_], rr.at[self.sems + sem], dev)
+
+        def end(self, there, sem):
+            for i, h, sem_ in ((0, 1, 3), (1, 0, 4), (0, 0, 2), (1, 1, 5)):
+                arrived(self.two.at[i, h], rr.at[self.sems + sem_])
+            other = self.place(y, 1 - xh)
+            add(
+                at_unit(y, 1 - xh), 2 * OWN, self.group,
+                self.two.at[0, 1 - xh], self.two.at[1, 1 - xh], to=other,
+            )
+            pass_on(other, there, sem, xp)
+            add(at_unit(y, xh), 2 * OWN, self.group, self.two.at[0, xh], self.two.at[1, xh])
+
+    def near_place(b, xh_):
+        chip = b * 2 + xh_
+        return xov.at[chip // 5, pl.ds(0, 2 * OWN), pl.ds(al((chip % 5) * PAIR, 128), PAIR)]
+
+    def rest_place(b, xh_):
+        return wb.at[unit(b, xh_), pl.ds(0, PAIR)]
+
+    along_near = AlongY(near, near_place, n1, n23, 0)
+    along_rest = AlongY(rest, rest_place, r1, r23, 6)
+
+    pl.when(s < 7)(lambda: arriving(0))
+    for b in (y2, yp, ym, y):
+        more(b, 0)
+        along_near.begin(b)
+
+    far_block(1 - xh, 1)
+    along_near.middle()
     for copy in w_sends + x_sends:
         copy.wait_send()
-
-    def unit(y_, xh_, n=2, first_=0):
-        return pl.ds(al((y_ * 2 + xh_) * 2 * OWN + first_ * OWN, 32), n * OWN)
-
-    def rounded(b):
-        @pl.loop(0, QUART // 32)
-        def _(r):
-            rows = pl.ds(al(b * QUART + r * 32, 32), 32)
-            wb[rows, pl.ds(0, HALF)] = acc[rows, :].astype(BF16)
-
-    def finish(b):
-        @pl.when(s < 7)
-        def _():
-            more(b, late)
-
-        rounded(b)
-
-    ycol, xcol = pl.ds(0, YW), pl.ds(YW, XW)
-    r_sends = []
-
-    def to_partner(b, n):
-        r_sends.append(send(wb.at[unit(b, 1 - xh), xcol], qx.at[n], rr.at[7 + n], xp))
-
-    finish(y2)
-    r_sends.append(send(wb.at[unit(y2, 0), ycol], r1.at[0], rr.at[0], up))
-    r_sends.append(send(wb.at[unit(y2, 1), ycol], r1.at[1], rr.at[1], down))
-    to_partner(y2, 0)
-    finish(yp)
-    r_sends.append(send(wb.at[unit(yp, 1), ycol], r23.at[0, 1], rr.at[3], up))
-    to_partner(yp, 1)
-    finish(ym)
-    r_sends.append(send(wb.at[unit(ym, 0), ycol], r23.at[1, 0], rr.at[4], down))
-    to_partner(ym, 2)
-    finish(y)
-    to_partner(y, 3)
+    pl.when(s < 7)(lambda: arriving(1))
+    mcol = pl.ds(PAIR, MIDS)
+
+    for n, b in enumerate((y2, yp, ym, y)):
+        more(b, 1)
+        along_rest.begin(b)
+        ref = wb.at[unit(b, 1 - xh), mcol]
+        add(at_unit(b, 1 - xh), 2 * OWN, mid, to=ref)
+        pass_on(ref, qx.at[n], rr.at[14 + n], xp)
     n_sends = []
     for i in range(1, 16):
         e = (d + i) % 16
@@ -315,70 +366,45 @@
         )
 
 
-    def add(start, count, cols, *terms, to=None, keep=False):
-        @pl.loop(0, count // 32)
-        def _(r):
-            rows = pl.ds(al(start + r * 32, 32), 32)
-            total = acc[rows, cols]
-            for term in terms:
-                total += term[pl.ds(al(r * 32, 32), 32), :].astype(F32)
-            if keep:
-                acc[rows, cols] = total
-            else:
-                wb[rows, cols] = total.astype(BF16)
-
-    def at_unit(y_, xh_, c_=0):
-        return index(y_, xh_, c_) * OWN
-
-    arrived(r1.at[0], rr.at[0])
-    add(at_unit(yp, 0), 2 * OWN, ycol, r1.at[0])
-    r_sends.append(send(wb.at[unit(yp, 0), ycol], r23.at[0, 0], rr.at[2], up))
-    arrived(r1.at[1], rr.at[1])
-    add(at_unit(ym, 1), 2 * OWN, ycol, r1.at[1])
-    r_sends.append(send(wb.at[unit(ym, 1), ycol], r23.at[1, 1], rr.at[5], down))
-
-    arrived(qx.at[0], rr.at[7])
-    add(at_unit(y2, xh), 2 * OWN, xcol, qx.at[0])
-    r_sends.append(send(wb.at[unit(y2, xh, 1, 0), xcol], q1.at[0], rr.at[11], up))
-    r_sends.append(send(wb.at[unit(y2, xh, 1, 1), xcol], q1.at[1], rr.at[12], down))
-    arrived(qx.at[1], rr.at[8])
-    add(at_unit(yp, xh, 1), OWN, xcol, qx.at[1, pl.ds(OWN, OWN)])
-    r_sends.append(send(wb.at[unit(yp, xh, 1, 1), xcol], q23.at[0, 1], rr.at[14], up))
-    add(at_unit(yp, xh, 0), OWN, xcol, qx.at[1, pl.ds(0, OWN)], keep=True)
-    arrived(qx.at[2], rr.at[9])
-    add(at_unit(ym, xh, 0), OWN, xcol, qx.at[2, pl.ds(0, OWN)])
-    r_sends.append(send(wb.at[unit(ym, xh, 1, 0), xcol], q23.at[1, 0], rr.at[15], down))
-    add(at_unit(ym, xh, 1), OWN, xcol, qx.at[2, pl.ds(OWN, OWN)], keep=True)
+    along_rest.middle()
+    along_near.end(rx.at[0], rr.at[12])
+
+    def one_unit(y_, u):
+        return wb.at[unit(y_, xh, 1, u), mcol]
+
+    def mid_sum(y_, u, n):
+        return at_unit(y_, xh, u), OWN, mid, qx.at[n, pl.ds(u * OWN, OWN)]
+
+    arrived(qx.at[0], rr.at[14])
+    for u, dev in ((0, up), (1, down)):
+        add(*mid_sum(y2, u, 0), to=one_unit(y2, u))
+        pass_on(one_unit(y2, u), q1.at[u], rr.at[18 + u], dev)
+    arrived(qx.at[1], rr.at[15])
+    add(*mid_sum(yp, 1, 1), to=one_unit(yp, 1))
+    pass_on(one_unit(yp, 1), q23.at[0, 1], rr.at[21], up)
+    arrived(qx.at[2], rr.at[16])
+    add(*mid_sum(ym, 0, 2), to=one_unit(ym, 0))
+    pass_on(one_unit(ym, 0), q23.at[1, 0], rr.at[22], down)
     l_m = [load(first.at[:, half(h)], acc.at[unit(y2, h, 1, 0)], 7 + h) for h in range(2)]
     l_v = [load(second.at[:, half(h)], acc.at[unit(y2, h, 1, 1)], 9 + h) for h in range(2)]
-
-    arrived(r23.at[0, 1], rr.at[3])
-    arrived(r23.at[1, 0], rr.at[4])
-    arrived(r23.at[0, 0], rr.at[2])
-    arrived(r23.at[1, 1], rr.at[5])
-    arrived(qx.at[3], rr.at[10])
-    add(at_unit(y, 1 - xh), 2 * OWN, ycol, r23.at[0, 1 - xh], r23.at[1, 1 - xh])
-    r_sends.append(send(wb.at[unit(y, 1 - xh), ycol], rx, rr.at[6], xp))
-    add(at_unit(y, xh), 2 * OWN, ycol, r23.at[0, xh], r23.at[1, xh], keep=True)
-
-    arrived(q1.at[0], rr.at[11])
-    add(at_unit(yp, xh, 0), OWN, xcol, q1.at[0])
-    r_sends.append(send(wb.at[unit(yp, xh, 1, 0), xcol], q23.at[0, 0], rr.at[13], up))
-    arrived(q1.at[1], rr.at[12])
-    add(at_unit(ym, xh, 1), OWN, xcol, q1.at[1])
-    r_sends.append(send(wb.at[unit(ym, xh, 1, 1), xcol], q23.at[1, 1], rr.at[16], down))
+    arrived(q1.at[0], rr.at[18])
+    add(*mid_sum(yp, 0, 1), q1.at[0], to=one_unit(yp, 0))
+    pass_on(one_unit(yp, 0), q23.at[0, 0], rr.at[20], up)
+    arrived(q1.at[1], rr.at[19])
+    add(*mid_sum(ym, 1, 2), q1.at[1], to=one_unit(ym, 1))
+    pass_on(one_unit(ym, 1), q23.at[1, 1], rr.at[23], down)
+    along_rest.end(rx.at[1], rr.at[13])
+    arrived(qx.at[3], rr.at[17])
+    arrived(rx.at[0], rr.at[12])
+    add(at_unit(y, xh), 2 * OWN, rest, rx.at[0])
     for u in range(2):
-        arrived(q23.at[0, 1 - u], rr.at[13 + (1 - u)])
-        arrived(q23.at[1, u], rr.at[15 + u])
-    for u in range(2):
-        add(
-            at_unit(y, xh, u), OWN, xcol,
-            qx.at[3, pl.ds(u * OWN, OWN)], q23.at[0, u], q23.at[1, u], keep=True,
-        )
-    arrived(rx, rr.at[6])
-    add(at_unit(y, xh), 2 * OWN, ycol, rx, keep=True)
-
-    r_sends.append(send(acc.at[pl.ds(al(at_unit(y, xh, 1 - c), 32), OWN)], gx, rr.at[17], sib))
+        arrived(q23.at[0, u], rr.at[20 + u])
+        arrived(q23.at[1, u], rr.at[22 + u])
+        add(*mid_sum(y, u, 3), q23.at[0, u], q23.at[1, u])
+    arrived(rx.at[1], rr.at[13])
+    add(at_unit(y, xh), 2 * OWN, near, rx.at[1])
+
+    r_sends.append(send(acc.at[pl.ds(al(at_unit(y, xh, 1 - c), 32), OWN)], gx, rr.at[24], sib))
 
     @pl.loop(0, 256 // 32)
     def _(r):
@@ -413,7 +439,7 @@
         stores.append(load(acc.at[unit(y2, which, 1, 1)], out_v.at[:, half(which)], n + 2))
 
     adam(c, acc, at_unit(y, xh, c))
-    arrived(gx, rr.at[17])
+    arrived(gx, rr.at[24])
     adam(1 - c, gx, 0)
 
     l_ni.wait()
@@ -530,12 +556,14 @@
             vm((4, ROWS, QUART), BF16),
             vm((2, 2, ROWS, QUART), BF16),
             vm((512, 256), BF16),
-            vm((2, 2 * OWN, YW), BF16),
-            vm((2, 2, 2 * OWN, YW), BF16),
-            vm((2 * OWN, YW), BF16),
-            vm((4, 2 * OWN, XW), BF16),
-            vm((2, OWN, XW), BF16),
-            vm((2, 2, OWN, XW), BF16),
+            vm((2, 2 * OWN, PAIR), BF16),
+            vm((2, 2, 2 * OWN, PAIR), BF16),
+            vm((2, 2 * OWN, PAIR), BF16),
+            vm((2, 2, 2 * OWN, PAIR), BF16),
+            vm((2, 2 * OWN, PAIR), BF16),
+            vm((4, 2 * OWN, MIDS), BF16),
+            vm((2, OWN, MIDS), BF16),
+            vm((2, 2, OWN, MIDS), BF16),
             vm((OWN, HALF), F32),
             vm((256, FEAT), BF16),
             vm((8, 32, FEAT), BF16),
@@ -547,7 +575,7 @@
             dma((4,)),
             dma((16,)),
             dma((2, 2, 2, 2)),
-            dma((18,)),
+            dma((25,)),
             dma((4,)),
             dma((8,)),
         ],

time: 159 us -> 151 us (0.950)
  Pallas kernels: 158 us -> 150 us
    pallas_call x1, Pallas kernels: 154 us -> 146 us  [step(): pl.pallas_call(kernel, out_shape=(shape((OWN, FEAT), F32), shape((OWN, FE...]
where the time goes in v3:
time: 151 us
  Pallas kernels  150 us (99%)
    pallas_call x1, Pallas kernels, step(): pl.pallas_call(kernel, out_shape=(shape((OWN, FEAT), F32), shape((OWN, FE...  146 us
    pallas_call x1, Pallas kernels, settle(): pl.pallas_call(settle_kernel, out_shape=tuple((jax.ShapeDtypeStruct(v.sha...  3.79 us

profile of v3, /device:TPU:1, one launch (start us, length us, event | category | flops | bytes accessed | tf_op | source)
XLA Modules:
  0.0 150.5 jit_solution(8623265193202614057)
XLA Ops:
  0.6 145.9 %section_step.1 = (f32[160,2560]{1,0:T(8,128)}, f32[160,2560]{1,0:T(8,128)}, f32[160,2560]{1,0:T(8,128)}, bf16[32,2560]{1,0:T(8,128)(2,1)}) custom-call(f32[160,2560]{1,0:T(8,128)} %bitcast.16, f32[160,2560]{1,0:T(8,128)} %bitcast.17, f32[160,2560]{1,0:T(8,128)} %bitcast.18, bf16[512,2560]{1,0:T(8,128)(2,1)} %bitcast.13, bf16[512,2560]{1,0:T(8,128)(2,1)} %bitcast.14, ...), custom_call_target="tpu_custom_call" | custom-call | tf_op jit(solution)/shard_map/section_step/pallas_call | solution.py:535
  146.5 3.8 %settle.1 = (f32[160,2560]{1,0:T(8,128)}, f32[160,2560]{1,0:T(8,128)}, f32[160,2560]{1,0:T(8,128)}, bf16[32,2560]{1,0:T(8,128)(2,1)}) custom-call(f32[160,2560]{1,0:T(8,128)} %get-tuple-element.12.refs_0_, f32[160,2560]{1,0:T(8,128)} %get-tuple-element.13.refs_1_, f32[160,2560]{1,0:T(8,128)} %get-tuple-element.14.refs_2_, ...), custom_call_target="tpu_custom_call" | custom-call | tf_op jit(solution)/shard_map/settle/pallas_call | solution.py:518

commit v4 on v3

--- a/solution.py
+++ b/solution.py
@@ -169,11 +169,13 @@
     arrived(owner(y, xh, 1 - c), ws.at[0])
     outgoing(y, 0, 0)
     piece = owner(ym, xh, c)
-    relay(1, piece, (owner(ym, xh, c, 0, 80), wr.at[5], up), (piece, ws.at[2], sib))
+    relay(1, piece, (owner(ym, xh, c, 0, 80), wr.at[5], up))
     piece = owner(yp, xh, c)
-    relay(2, piece, (owner(yp, xh, c, 80, 80), wr.at[6], down), (piece, ws.at[3], sib))
+    relay(2, piece, (owner(yp, xh, c, 80, 80), wr.at[6], down))
     piece = owner(y, 1 - xh, c)
-    relay(0, piece, (piece, wr.at[3], up), (piece, wr.at[4], down), (piece, ws.at[1], sib))
+    relay(0, piece, (piece, ws.at[1], sib), (piece, wr.at[3], up), (piece, wr.at[4], down))
+    for piece, i in ((owner(ym, xh, c), 2), (owner(yp, xh, c), 3)):
+        w_sends.append(send(piece, piece, ws.at[i], sib))
     arrived(owner(y, 1 - xh, 1 - c), ws.at[1])
     outgoing(y, 0, 1)
     arrived(owner(ym, xh, 1 - c), ws.at[2])
@@ -353,6 +355,8 @@
         ref = wb.at[unit(b, 1 - xh), mcol]
         add(at_unit(b, 1 - xh), 2 * OWN, mid, to=ref)
         pass_on(ref, qx.at[n], rr.at[14 + n], xp)
+    along_rest.middle()
+    along_near.end(rx.at[0], rr.at[12])
     n_sends = []
     for i in range(1, 16):
         e = (d + i) % 16
@@ -365,9 +369,6 @@
             )
         )
 
-
-    along_rest.middle()
-    along_near.end(rx.at[0], rr.at[12])
 
     def one_unit(y_, u):
         return wb.at[unit(y_, xh, 1, u), mcol]
@@ -387,13 +388,13 @@
     pass_on(one_unit(ym, 0), q23.at[1, 0], rr.at[22], down)
     l_m = [load(first.at[:, half(h)], acc.at[unit(y2, h, 1, 0)], 7 + h) for h in range(2)]
     l_v = [load(second.at[:, half(h)], acc.at[unit(y2, h, 1, 1)], 9 + h) for h in range(2)]
+    along_rest.end(rx.at[1], rr.at[13])
     arrived(q1.at[0], rr.at[18])
     add(*mid_sum(yp, 0, 1), q1.at[0], to=one_unit(yp, 0))
     pass_on(one_unit(yp, 0), q23.at[0, 0], rr.at[20], up)
     arrived(q1.at[1], rr.at[19])
     add(*mid_sum(ym, 1, 2), q1.at[1], to=one_unit(ym, 1))
     pass_on(one_unit(ym, 1), q23.at[1, 1], rr.at[23], down)
-    along_rest.end(rx.at[1], rr.at[13])
     arrived(qx.at[3], rr.at[17])
     arrived(rx.at[0], rr.at[12])
     add(at_unit(y, xh), 2 * OWN, rest, rx.at[0])
@@ -438,44 +439,48 @@
         stores.append(load(acc.at[unit(y2, which, 1, 0)], out_m.at[:, half(which)], n + 1))
         stores.append(load(acc.at[unit(y2, which, 1, 1)], out_v.at[:, half(which)], n + 2))
 
-    adam(c, acc, at_unit(y, xh, c))
-    arrived(gx, rr.at[24])
-    adam(1 - c, gx, 0)
-
     l_ni.wait()
     for i in range(1, 16):
         e = (d - i + 16) % 16
         arrived(niw.at[pl.ds(al((e % 2) * 256 + (e // 2) * 32, 32), 32)], nr.at[i])
     c_sends = []
-    for q in range(4):
-        cols = pl.ds(q * QUART, QUART)
-        gv[pl.ds(0, 256), cols] = jnp.dot(
-            niw[pl.ds(al((1 - c) * 256, 256), 256), :],
-            mo[pl.ds(0, 256), cols],
-            preferred_element_type=F32,
-        ).astype(BF16)
-        c_sends.append(send(gv.at[pl.ds(0, 256), cols], cz.at[:, cols], zr.at[q], sib))
-    for q in range(4):
-        cols = pl.ds(q * QUART, QUART)
-        total = jnp.dot(
-            niw[pl.ds(al(c * 256, 256), 256), :],
+
+    def product(c_, cols):
+        return jnp.dot(
+            niw[pl.ds(al(c_ * 256, 256), 256), :],
             mo[pl.ds(0, 256), cols],
             preferred_element_type=F32,
         )
-        arrived(cz.at[:, cols], zr.at[q])
+
+    order = [(h, q, pl.ds(al(which * HALF + q * QUART, 128), QUART))
+             for h, which in enumerate((c, 1 - c)) for q in range(2)]
+    for turn, (which, gradient, start) in enumerate(((c, acc, at_unit(y, xh, c)), (1 - c, gx, 0))):
+        if turn == 1:
+            arrived(gx, rr.at[24])
+        adam(which, gradient, start)
+        for h, q, cols in order:
+            if h == turn:
+                gv[pl.ds(0, 256), cols] = product(1 - c, cols).astype(BF16)
+                c_sends.append(
+                    send(gv.at[pl.ds(0, 256), cols], cz.at[:, cols], zr.at[(1 - h) * 2 + q], sib)
+                )
+    for h, q, cols in reversed(order):
+        total = product(c, cols)
+        arrived(cz.at[:, cols], zr.at[h * 2 + q])
         gv[pl.ds(256, 256), cols] = (total + cz[:, cols].astype(F32)).astype(BF16)
-    for i in range(1, 8):
-        e = (k + i) % 8
-        c_sends.append(
-            send(
-                gv.at[pl.ds(al(256 + e * 32, 32), 32)],
-                cr.at[i],
-                cs.at[i],
-                (s, e * 2 + c),
+        for i in range(1, 8):
+            e = (k + i) % 8
+            c_sends.append(
+                send(
+                    gv.at[pl.ds(al(256 + e * 32, 32), 32), cols],
+                    cr.at[i, :, cols],
+                    cs.at[i, h * 2 + q],
+                    (s, e * 2 + c),
+                )
             )
-        )
-    for i in range(1, 8):
-        arrived(cr.at[i], cs.at[i])
+    for h, q, cols in reversed(order):
+        for i in range(1, 8):
+            arrived(cr.at[i, :, cols], cs.at[i, h * 2 + q])
 
     @pl.loop(0, 2)
     def _(r):
@@ -569,7 +574,7 @@
             vm((8, 32, FEAT), BF16),
             vm((32, FEAT), BF16),
             dma((18,)),
-            dma((112,)),
+            dma((160,)),
             dma((9,)),
             dma((10,)),
             dma((4,)),
@@ -577,7 +582,7 @@
             dma((2, 2, 2, 2)),
             dma((25,)),
             dma((4,)),
-            dma((8,)),
+            dma((8, 4)),
         ],
         compiler_params=pltpu.CompilerParams(
             collective_id=0, has_side_effects=True, vmem_limit_bytes=67043328

time: 151 us -> 149 us (0.987)
  Pallas kernels: 150 us -> 148 us
    pallas_call x1, Pallas kernels: 146 us -> 144 us  [step(): pl.pallas_call(kernel, out_shape=(shape((OWN, FEAT), F32), shape((OWN, FE...]
where the time goes in v4:
time: 149 us; the launch traced here: 148 us
  Pallas kernels  148 us (99%)
    pallas_call x1, Pallas kernels, step(): pl.pallas_call(kernel, out_shape=(shape((OWN, FEAT), F32), shape((OWN, FE...  144 us
    pallas_call x1, Pallas kernels, settle(): pl.pallas_call(settle_kernel, out_shape=tuple((jax.ShapeDtypeStruct(v.sha...  3.79 us

profile of v4, /device:TPU:1, one launch (start us, length us, event | category | flops | bytes accessed | tf_op | source)
XLA Modules:
  0.0 148.4 jit_solution(16812358634065824099)
XLA Ops:
  0.6 143.8 %section_step.1 = (f32[160,2560]{1,0:T(8,128)}, f32[160,2560]{1,0:T(8,128)}, f32[160,2560]{1,0:T(8,128)}, bf16[32,2560]{1,0:T(8,128)(2,1)}) custom-call(f32[160,2560]{1,0:T(8,128)} %bitcast.16, f32[160,2560]{1,0:T(8,128)} %bitcast.17, f32[160,2560]{1,0:T(8,128)} %bitcast.18, bf16[512,2560]{1,0:T(8,128)(2,1)} %bitcast.13, bf16[512,2560]{1,0:T(8,128)(2,1)} %bitcast.14, ...), custom_call_target="tpu_custom_call" | custom-call | tf_op jit(solution)/shard_map/section_step/pallas_call | solution.py:540
  144.5 3.8 %settle.1 = (f32[160,2560]{1,0:T(8,128)}, f32[160,2560]{1,0:T(8,128)}, f32[160,2560]{1,0:T(8,128)}, bf16[32,2560]{1,0:T(8,128)(2,1)}) custom-call(f32[160,2560]{1,0:T(8,128)} %get-tuple-element.12.refs_0_, f32[160,2560]{1,0:T(8,128)} %get-tuple-element.13.refs_1_, f32[160,2560]{1,0:T(8,128)} %get-tuple-element.14.refs_2_, ...), custom_call_target="tpu_custom_call" | custom-call | tf_op jit(solution)/shard_map/settle/pallas_call | solution.py:523

commit v5 on v4

--- a/solution.py
+++ b/solution.py
@@ -389,98 +389,129 @@
     l_m = [load(first.at[:, half(h)], acc.at[unit(y2, h, 1, 0)], 7 + h) for h in range(2)]
     l_v = [load(second.at[:, half(h)], acc.at[unit(y2, h, 1, 1)], 9 + h) for h in range(2)]
     along_rest.end(rx.at[1], rr.at[13])
+
+    @pl.loop(0, 256 // 32)
+    def _(r):
+        mo[pl.ds(al(r * 32, 32), 32), :] = jnp.zeros((32, FEAT), BF16)
+
     arrived(q1.at[0], rr.at[18])
     add(*mid_sum(yp, 0, 1), q1.at[0], to=one_unit(yp, 0))
     pass_on(one_unit(yp, 0), q23.at[0, 0], rr.at[20], up)
     arrived(q1.at[1], rr.at[19])
     add(*mid_sum(ym, 1, 2), q1.at[1], to=one_unit(ym, 1))
     pass_on(one_unit(ym, 1), q23.at[1, 1], rr.at[23], down)
+
+    shift = (d % 4) * 32
+    stores, c_sends = [], []
+
+    def zone(n, xh_):
+        return (((1 - xh_) * 384, PART), (xh_ * 256, PART + MID))[n]
+
+    def exchanged(n, j):
+        width = (PART, PART + MID)[n]
+        return pl.ds(n * PAIR + j * width, width)
+
+    def adam(which, n):
+        begin, width = zone(n, xh)
+
+        @pl.loop(0, OWN // 16)
+        def _(r):
+            here = pl.ds(al(r * 16, 16), 16)
+            at_m = pl.ds(al(at_unit(y2, which, 0) + r * 16, 16), 16)
+            at_v = pl.ds(al(at_unit(y2, which, 1) + r * 16, 16), 16)
+            for j in range(2):
+                local = pl.ds(al(j * QUART + begin, 128), width)
+                cols = pl.ds(al(which * HALF + j * QUART + begin, 128), width)
+                if which is c:
+                    g = acc[pl.ds(al(at_unit(y, xh, c) + r * 16, 16), 16), local]
+                else:
+                    g = gx[here, exchanged(n, j)]
+                params = mst[here, cols]
+                m = FIRST_DECAY * acc[at_m, local] + (1.0 - FIRST_DECAY) * g
+                v = SECOND_DECAY * acc[at_v, local] + (1.0 - SECOND_DECAY) * g * g
+                acc[at_m, local] = m
+                acc[at_v, local] = v
+                direction = m / FIRST_CORRECTION / (jnp.sqrt(v / SECOND_CORRECTION) + EPSILON)
+                new = params - LEARN_RATE * (direction + WEIGHT_DECAY * params)
+                mst[here, cols] = new
+                mo[pl.ds(al(shift + r * 16, 16), 16), cols] = new.astype(BF16)
+
+    def product(c_, cols):
+        return jnp.dot(
+            niw[pl.ds(al(c_ * 256, 256), 256), :],
+            mo[pl.ds(0, 256), cols],
+            preferred_element_type=F32,
+        )
+
+    def slices(n, xh_):
+        begin, width = zone(n, xh_)
+        return [
+            (h, j, pl.ds(al(which * HALF + j * QUART + begin, 128), width))
+            for h, which in enumerate((c, 1 - c))
+            for j in range(2)
+        ]
+
+    def update(n):
+        begin, width = zone(n, xh)
+        theirs = pl.ds(al(at_unit(y, xh, 1 - c), 32), OWN)
+        for j in range(2):
+            pass_on(
+                acc.at[theirs, pl.ds(al(j * QUART + begin, 128), width)],
+                gx.at[:, exchanged(n, j)],
+                rr.at[24 + 2 * n + j],
+                sib,
+            )
+        if n == 0:
+            for copy in l_m + l_v:
+                copy.wait()
+            l_ni.wait()
+            for i in range(1, 16):
+                e = (d - i + 16) % 16
+                arrived(niw.at[pl.ds(al((e % 2) * 256 + (e // 2) * 32, 32), 32)], nr.at[i])
+        for turn, which in enumerate((c, 1 - c)):
+            if turn == 1:
+                for j in range(2):
+                    arrived(gx.at[:, exchanged(n, j)], rr.at[24 + 2 * n + j])
+            adam(which, n)
+            for h, j, cols in slices(n, xh):
+                if h == turn:
+                    gv[pl.ds(0, 256), cols] = product(1 - c, cols).astype(BF16)
+                    sem = zr.at[n * 4 + (1 - h) * 2 + j]
+                    c_sends.append(send(gv.at[pl.ds(0, 256), cols], cz.at[:, cols], sem, sib))
+        for h, j, cols in reversed(slices(n, xh)):
+            total = product(c, cols)
+            arrived(cz.at[:, cols], zr.at[n * 4 + h * 2 + j])
+            gv[pl.ds(256, 256), cols] = (total + cz[:, cols].astype(F32)).astype(BF16)
+            for i in range(1, 8):
+                e = (k + i) % 8
+                c_sends.append(
+                    send(
+                        gv.at[pl.ds(al(256 + e * 32, 32), 32), cols],
+                        cr.at[i, :, cols],
+                        cs.at[i, n * 4 + h * 2 + j],
+                        (s, e * 2 + c),
+                    )
+                )
+
     arrived(qx.at[3], rr.at[17])
     arrived(rx.at[0], rr.at[12])
     add(at_unit(y, xh), 2 * OWN, rest, rx.at[0])
+    update(0)
     for u in range(2):
         arrived(q23.at[0, u], rr.at[20 + u])
         arrived(q23.at[1, u], rr.at[22 + u])
         add(*mid_sum(y, u, 3), q23.at[0, u], q23.at[1, u])
     arrived(rx.at[1], rr.at[13])
     add(at_unit(y, xh), 2 * OWN, near, rx.at[1])
-
-    r_sends.append(send(acc.at[pl.ds(al(at_unit(y, xh, 1 - c), 32), OWN)], gx, rr.at[24], sib))
-
-    @pl.loop(0, 256 // 32)
-    def _(r):
-        mo[pl.ds(al(r * 32, 32), 32), :] = jnp.zeros((32, FEAT), BF16)
-
-    for copy in l_m + l_v:
-        copy.wait()
-    shift = (d % 4) * 32
-    stores = []
-
-    def adam(which, gradient, start):
-        @pl.loop(0, OWN // 16)
-        def _(r):
-            here = pl.ds(al(r * 16, 16), 16)
-            cols = half(which)
-            at_m = pl.ds(al(at_unit(y2, which, 0) + r * 16, 16), 16)
-            at_v = pl.ds(al(at_unit(y2, which, 1) + r * 16, 16), 16)
-            g = gradient[pl.ds(al(start + r * 16, 16), 16), :]
-            params = mst[here, cols]
-            m = FIRST_DECAY * acc[at_m, :] + (1.0 - FIRST_DECAY) * g
-            v = SECOND_DECAY * acc[at_v, :] + (1.0 - SECOND_DECAY) * g * g
-            acc[at_m, :] = m
-            acc[at_v, :] = v
-            direction = m / FIRST_CORRECTION / (jnp.sqrt(v / SECOND_CORRECTION) + EPSILON)
-            new = params - LEARN_RATE * (direction + WEIGHT_DECAY * params)
-            mst[here, cols] = new
-            mo[pl.ds(al(shift + r * 16, 16), 16), cols] = new.astype(BF16)
-
-        n = 11 if which is c else 14
-        stores.append(load(mst.at[:, half(which)], out_p.at[:, half(which)], n))
-        stores.append(load(acc.at[unit(y2, which, 1, 0)], out_m.at[:, half(which)], n + 1))
-        stores.append(load(acc.at[unit(y2, which, 1, 1)], out_v.at[:, half(which)], n + 2))
-
-    l_ni.wait()
-    for i in range(1, 16):
-        e = (d - i + 16) % 16
-        arrived(niw.at[pl.ds(al((e % 2) * 256 + (e // 2) * 32, 32), 32)], nr.at[i])
-    c_sends = []
-
-    def product(c_, cols):
-        return jnp.dot(
-            niw[pl.ds(al(c_ * 256, 256), 256), :],
-            mo[pl.ds(0, 256), cols],
-            preferred_element_type=F32,
-        )
-
-    order = [(h, q, pl.ds(al(which * HALF + q * QUART, 128), QUART))
-             for h, which in enumerate((c, 1 - c)) for q in range(2)]
-    for turn, (which, gradient, start) in enumerate(((c, acc, at_unit(y, xh, c)), (1 - c, gx, 0))):
-        if turn == 1:
-            arrived(gx, rr.at[24])
-        adam(which, gradient, start)
-        for h, q, cols in order:
-            if h == turn:
-                gv[pl.ds(0, 256), cols] = product(1 - c, cols).astype(BF16)
-                c_sends.append(
-                    send(gv.at[pl.ds(0, 256), cols], cz.at[:, cols], zr.at[(1 - h) * 2 + q], sib)
-                )
-    for h, q, cols in reversed(order):
-        total = product(c, cols)
-        arrived(cz.at[:, cols], zr.at[h * 2 + q])
-        gv[pl.ds(256, 256), cols] = (total + cz[:, cols].astype(F32)).astype(BF16)
+    update(1)
+    for h in range(2):
+        stores.append(load(mst.at[:, half(h)], out_p.at[:, half(h)], 11 + h))
+        stores.append(load(acc.at[unit(y2, h, 1, 0)], out_m.at[:, half(h)], 13 + h))
+        stores.append(load(acc.at[unit(y2, h, 1, 1)], out_v.at[:, half(h)], 15 + h))
+    for n in range(2):
         for i in range(1, 8):
-            e = (k + i) % 8
-            c_sends.append(
-                send(
-                    gv.at[pl.ds(al(256 + e * 32, 32), 32), cols],
-                    cr.at[i, :, cols],
-                    cs.at[i, h * 2 + q],
-                    (s, e * 2 + c),
-                )
-            )
-    for h, q, cols in reversed(order):
-        for i in range(1, 8):
-            arrived(cr.at[i, :, cols], cs.at[i, h * 2 + q])
+            for h, j, cols in slices(n, (k - i + 8) % 2):
+                arrived(cr.at[i, :, cols], cs.at[i, n * 4 + h * 2 + j])
 
     @pl.loop(0, 2)
     def _(r):
@@ -507,8 +538,13 @@
 def settle_kernel(*refs):
     count = len(refs) // 4
     sources, targets, held, sems = (refs[i * count : (i + 1) * count] for i in range(4))
-    taken = [pltpu.make_async_copy(a, v, m.at[0]) for a, v, m in zip(sources, held, sems)]
-    given = [pltpu.make_async_copy(v, b, m.at[1]) for v, b, m in zip(held, targets, sems)]
+    taken, given = [], []
+    for source, target, middle, sem in zip(sources, targets, held, sems):
+        height = source.shape[0] // 4 if source.shape[0] == OWN else source.shape[0]
+        for i in range(source.shape[0] // height):
+            rows = pl.ds(i * height, height)
+            taken.append(pltpu.make_async_copy(source.at[rows], middle.at[rows], sem.at[0, i]))
+            given.append(pltpu.make_async_copy(middle.at[rows], target.at[rows], sem.at[1, i]))
     for copy in taken:
         copy.start()
     for copy, onward in zip(taken, given):
@@ -526,7 +562,7 @@
         in_specs=[anywhere] * len(values),
         out_specs=[anywhere] * len(values),
         scratch_shapes=[pltpu.VMEM(v.shape, v.dtype) for v in values]
-        + [pltpu.SemaphoreType.DMA((2,)) for _ in values],
+        + [pltpu.SemaphoreType.DMA((2, 4)) for _ in values],
         name="settle",
     )(*values)
 
@@ -574,15 +610,15 @@
             vm((8, 32, FEAT), BF16),
             vm((32, FEAT), BF16),
             dma((18,)),
-            dma((160,)),
+            dma((224,)),
             dma((9,)),
             dma((10,)),
             dma((4,)),
             dma((16,)),
             dma((2, 2, 2, 2)),
-            dma((25,)),
-            dma((4,)),
-            dma((8, 4)),
+            dma((28,)),
+            dma((8,)),
+            dma((8, 8)),
         ],
         compiler_params=pltpu.CompilerParams(
             collective_id=0, has_side_effects=True, vmem_limit_bytes=67043328

time: 149 us -> 144 us (0.966)
  Pallas kernels: 148 us -> 143 us
    pallas_call x1, Pallas kernels: 144 us -> 138 us  [step(): pl.pallas_call(kernel, out_shape=(shape((OWN, FEAT), F32), shape((OWN, FE...]
where the time goes in v5:
time: 144 us
  Pallas kernels  143 us (99%)
    pallas_call x1, Pallas kernels, step(): pl.pallas_call(kernel, out_shape=(shape((OWN, FEAT), F32), shape((OWN, FE...  138 us
    pallas_call x1, Pallas kernels, settle(): pl.pallas_call(settle_kernel, out_shape=tuple((jax.ShapeDtypeStruct(v.sha...  4.42 us

profile of v5, /device:TPU:1, one launch (start us, length us, event | category | flops | bytes accessed | tf_op | source)
XLA Modules:
  0.0 143.5 jit_solution(13772279596638729738)
XLA Ops:
  0.6 138.3 %section_step.1 = (f32[160,2560]{1,0:T(8,128)}, f32[160,2560]{1,0:T(8,128)}, f32[160,2560]{1,0:T(8,128)}, bf16[32,2560]{1,0:T(8,128)(2,1)}) custom-call(f32[160,2560]{1,0:T(8,128)} %bitcast.16, f32[160,2560]{1,0:T(8,128)} %bitcast.17, f32[160,2560]{1,0:T(8,128)} %bitcast.18, bf16[512,2560]{1,0:T(8,128)(2,1)} %bitcast.13, bf16[512,2560]{1,0:T(8,128)(2,1)} %bitcast.14, ...), custom_call_target="tpu_custom_call" | custom-call | tf_op jit(solution)/shard_map/section_step/pallas_call | solution.py:576
  138.9 4.4 %settle.1 = (f32[160,2560]{1,0:T(8,128)}, f32[160,2560]{1,0:T(8,128)}, f32[160,2560]{1,0:T(8,128)}, bf16[32,2560]{1,0:T(8,128)(2,1)}) custom-call(f32[160,2560]{1,0:T(8,128)} %get-tuple-element.12.refs_0_, f32[160,2560]{1,0:T(8,128)} %get-tuple-element.13.refs_1_, f32[160,2560]{1,0:T(8,128)} %get-tuple-element.14.refs_2_, ...), custom_call_target="tpu_custom_call" | custom-call | tf_op jit(solution)/shard_map/settle/pallas_call | solution.py:559

commit v6 on v5

--- a/solution.py
+++ b/solution.py
@@ -85,8 +85,8 @@
     )
 
     barrier = pltpu.get_barrier_semaphore()
-    for i in range(1, 16):
-        pl.semaphore_signal(barrier, inc=1, device_id=(s, (d + i) % 16), device_id_type=MESH)
+    for dev in (up, down, xp, sib):
+        pl.semaphore_signal(barrier, inc=1, device_id=dev, device_id_type=MESH)
 
     @pl.when(s > 0)
     def _():
@@ -104,7 +104,7 @@
     def _(r):
         wb[pl.ds(al(d * OWN + r * 16, 16), 16), :] = mst[pl.ds(al(r * 16, 16), 16), :].astype(BF16)
 
-    pl.semaphore_wait(barrier, 15 + 2 * jnp.minimum(s, 1) + 2 * jnp.minimum(7 - s, 1))
+    pl.semaphore_wait(barrier, 4 + 2 * jnp.minimum(s, 1) + 2 * jnp.minimum(7 - s, 1))
 
     mine = owner(y, xh, c)
     w_sends = [

time: 144 us -> 143 us (level)
  no operation moved by 1% of the time
where the time goes in v6:
time: 143 us
  Pallas kernels  142 us (99%)
    pallas_call x1, Pallas kernels, step(): pl.pallas_call(kernel, out_shape=(shape((OWN, FEAT), F32), shape((OWN, FE...  138 us
    pallas_call x1, Pallas kernels, settle(): pl.pallas_call(settle_kernel, out_shape=tuple((jax.ShapeDtypeStruct(v.sha...  4.42 us

profile of v6, /device:TPU:1, one launch (start us, length us, event | category | flops | bytes accessed | tf_op | source)
XLA Modules:
  0.0 143.0 jit_solution(7611565177890913849)
XLA Ops:
  0.6 137.7 %section_step.1 = (f32[160,2560]{1,0:T(8,128)}, f32[160,2560]{1,0:T(8,128)}, f32[160,2560]{1,0:T(8,128)}, bf16[32,2560]{1,0:T(8,128)(2,1)}) custom-call(f32[160,2560]{1,0:T(8,128)} %bitcast.16, f32[160,2560]{1,0:T(8,128)} %bitcast.17, f32[160,2560]{1,0:T(8,128)} %bitcast.18, bf16[512,2560]{1,0:T(8,128)(2,1)} %bitcast.13, bf16[512,2560]{1,0:T(8,128)(2,1)} %bitcast.14, ...), custom_call_target="tpu_custom_call" | custom-call | tf_op jit(solution)/shard_map/section_step/pallas_call | solution.py:576
  138.4 4.4 %settle.1 = (f32[160,2560]{1,0:T(8,128)}, f32[160,2560]{1,0:T(8,128)}, f32[160,2560]{1,0:T(8,128)}, bf16[32,2560]{1,0:T(8,128)(2,1)}) custom-call(f32[160,2560]{1,0:T(8,128)} %get-tuple-element.12.refs_0_, f32[160,2560]{1,0:T(8,128)} %get-tuple-element.13.refs_1_, f32[160,2560]{1,0:T(8,128)} %get-tuple-element.14.refs_2_, ...), custom_call_target="tpu_custom_call" | custom-call | tf_op jit(solution)/shard_map/settle/pallas_call | solution.py:559
